TPU v7x, 32 devices: a whole 2x2x4 slice. The times are simulated.
32 devices in a mesh: seq: 2 (over x), fsdp: 16 (over z, y, core).
Axes of the slice: x: 2, y: 2, z: 4, core: 2. Of those that a mesh axis runs over, the one named last changes fastest.
Arguments:
- tokens: bfloat16 [4096, 1024], P(('fsdp', 'seq')), may hold values from -6 to 6
- cotangent: bfloat16 [4096, 1024], P(('fsdp', 'seq')), may hold values from -6 to 6
- documents: int32 [16, 256], P('fsdp'), may hold values from 0 to 3, never falling along the last dimension, each value on 1 to 128 neighbouring positions
- in_weight: bfloat16 [1024, 4384], P('fsdp'), may hold values from -0.1875 to 0.1875
- kernel_taps: float32 [4, 2304], replicated, may hold values from -3 to 3
- kernel_bias: float32 [2304], replicated, may hold values from -0.5 to 0.5
- step_bias: float32 [32], replicated, may hold values from -6 to -2
- decay_log: float32 [32], replicated, may hold values from 0 to 2.77
- skip_gain: float32 [32], replicated, may hold values from 0.5 to 1.5
- pre_gain: float32 [1024], replicated, may hold values from 0.5 to 1.5
- norm_gain: float32 [2048], replicated, may hold values from 0.5 to 1.5
- out_weight: bfloat16 [2048, 1024], P('fsdp'), may hold values from -0.125 to 0.125
Outputs:
- block_output: bfloat16 [4096, 1024], P(('fsdp', 'seq'))
- tokens_grad: float32 [4096, 1024], P(('fsdp', 'seq'))
- in_weight_grad: float32 [1024, 4384], P('fsdp')
- kernel_taps_grad: float32 [4, 2304], replicated
- kernel_bias_grad: float32 [2304], replicated
- step_bias_grad: float32 [32], replicated
- decay_log_grad: float32 [32], replicated
- skip_gain_grad: float32 [32], replicated
- pre_gain_grad: float32 [1024], replicated
- norm_gain_grad: float32 [2048], replicated
- out_weight_grad: float32 [2048, 1024], P('fsdp')
Inputs may be any that keep to these rules, and one draw needn't show every extreme that they name: `documents`: in every sequence the ids start at 0 and never fall; each id marks one document of consecutive tokens, and every id of 0 to 3 occurs.
All inputs are finite; a program needn't handle non-finite values.
Results may differ from a plain program's by a relative error of at most 0.011.
Values may be sent and summed in bfloat16 or wider, within the bound.
A program may use at most 128 MiB of HBM per device.

v0:
```python
from functools import partial

import jax
import jax.numpy as jnp
from jax import lax
from jax.sharding import PartitionSpec as P

HEADS = 32
HEAD_DIM = 64
STATE = 128
CONV = 4
SPAN = 256
INNER = 2048
CONV_CH = 2304


norm_epsilon = 1e-05


def pre_norm(values, gain):
    scale = lax.rsqrt(jnp.mean(values * values, axis=-1, keepdims=True) + norm_epsilon)
    return values * scale * gain


def gate_norm(mixed, gates, gain):
    gated = mixed * jax.nn.silu(gates)
    scale = lax.rsqrt(jnp.mean(gated * gated, axis=-1, keepdims=True) + norm_epsilon)
    return gated * scale * gain


def block_step(state, block):
    scaled, input_matrix, output_matrix, log_block, seg_block, prev_last = block
    width = seg_block.shape[0]
    cumul = jnp.cumsum(log_block, axis=0).T
    places = jnp.arange(width)
    causal = (places[:, None] >= places[None, :]) & (seg_block[:, None] == seg_block[None, :])
    log_gap = cumul[:, :, None] - cumul[:, None, :]
    decay = jnp.where(causal[None], jnp.exp(jnp.where(causal[None], log_gap, 0.0)), 0.0)
    scores = jnp.dot(output_matrix, input_matrix.T, precision=lax.Precision.HIGHEST)
    inside = jnp.einsum(
        "hij,jhp->ihp", decay * scores[None], scaled, precision=lax.Precision.HIGHEST
    )
    entering = jnp.exp(cumul) * (seg_block == prev_last).astype(jnp.float32)[None]
    carried = (
        jnp.einsum("in,hnp->ihp", output_matrix, state, precision=lax.Precision.HIGHEST)
        * entering.T[:, :, None]
    )
    final = cumul[:, -1]
    leaving = (
        jnp.exp(final[:, None] - cumul) * (seg_block == seg_block[-1]).astype(jnp.float32)[None]
    )
    fresh = jnp.einsum(
        "hj,jn,jhp->hnp", leaving, input_matrix, scaled, precision=lax.Precision.HIGHEST
    )
    keeping = jnp.exp(final) * (seg_block[-1] == prev_last).astype(jnp.float32)
    new_state = keeping[:, None, None] * state + fresh
    return (new_state, inside + carried)


def mixer(segment, conv_in, step_raw, taps, tap_bias, bias_steps, log_rates, skips):
    length, channels = conv_in.shape
    heads = step_raw.shape[1]
    width = heads * HEAD_DIM
    summed = tap_bias + conv_in * taps[CONV - 1]
    for offset in range(1, CONV):
        shifted = jnp.concatenate(
            [jnp.zeros((offset, channels), jnp.float32), conv_in[: length - offset]], axis=0
        )
        matched = jnp.concatenate(
            [
                jnp.zeros((offset,), jnp.float32),
                (segment[offset:] == segment[: length - offset]).astype(jnp.float32),
            ]
        )
        summed = summed + taps[CONV - 1 - offset] * shifted * matched[:, None]
    active = jax.nn.silu(summed)
    values = active[:, :width].reshape(length, heads, HEAD_DIM)
    input_matrix = active[:, width : width + STATE]
    output_matrix = active[:, width + STATE :]
    steps_taken = jax.nn.softplus(step_raw + bias_steps)
    log_decay = steps_taken * -jnp.exp(log_rates)
    scaled = values * steps_taken[:, :, None]
    blocks = length // SPAN
    seg_blocks = segment.reshape(blocks, SPAN)
    prev_last = jnp.concatenate([seg_blocks[:1, 0], seg_blocks[:-1, -1]])
    initial = jnp.zeros((heads, STATE, HEAD_DIM), jnp.float32)
    _, outputs = lax.scan(
        block_step,
        initial,
        (
            scaled.reshape(blocks, SPAN, heads, HEAD_DIM),
            input_matrix.reshape(blocks, SPAN, STATE),
            output_matrix.reshape(blocks, SPAN, STATE),
            log_decay.reshape(blocks, SPAN, heads),
            seg_blocks,
            prev_last,
        ),
    )
    result = outputs.reshape(length, heads, HEAD_DIM) + values * skips[None, :, None]
    return result.reshape(length, width)


def local(
    tokens,
    cotangent,
    documents,
    in_weight,
    kernel_taps,
    kernel_bias,
    step_bias,
    decay_log,
    skip_gain,
    pre_gain,
    norm_gain,
    out_weight,
):
    group_count = lax.axis_size("seq")
    group_index = lax.axis_index("seq")
    local_heads = HEADS // group_count
    local_width = local_heads * HEAD_DIM
    head_start = group_index * local_width
    head_first = group_index * local_heads
    contract_rows = (((1,), (1,)), ((), ()))
    contract_tokens = (((0,), (0,)), ((), ()))
    floats = tokens.astype(jnp.float32)
    normed_in = pre_norm(floats, pre_gain).astype(jnp.bfloat16)
    in_whole = lax.all_gather(in_weight, "fsdp", axis=0, tiled=True)
    projected = jnp.dot(normed_in, in_whole, preferred_element_type=jnp.float32).astype(
        jnp.bfloat16
    )
    gates = projected[:, :INNER]
    values_raw = projected[:, INNER : 2 * INNER]
    state_raw = projected[:, 2 * INNER : INNER + CONV_CH]
    step_raw = projected[:, INNER + CONV_CH :]
    head_values, head_steps = (
        lax.all_to_all(values_raw, "seq", split_axis=1, concat_axis=0, tiled=True),
        lax.all_to_all(step_raw, "seq", split_axis=1, concat_axis=0, tiled=True),
    )
    state_whole = lax.all_gather(state_raw, "seq", axis=0, tiled=True)
    segment = documents[0]
    local_taps = jnp.concatenate(
        [lax.dynamic_slice_in_dim(kernel_taps, head_start, local_width, 1), kernel_taps[:, INNER:]],
        axis=1,
    )
    local_bias = jnp.concatenate(
        [lax.dynamic_slice_in_dim(kernel_bias, head_start, local_width, 0), kernel_bias[INNER:]],
        axis=0,
    )
    local_step_bias = lax.dynamic_slice_in_dim(step_bias, head_first, local_heads, 0)
    local_decay = lax.dynamic_slice_in_dim(decay_log, head_first, local_heads, 0)
    local_skip = lax.dynamic_slice_in_dim(skip_gain, head_first, local_heads, 0)
    conv_in = jnp.concatenate(
        [head_values.astype(jnp.float32), state_whole.astype(jnp.float32)], axis=1
    )
    mixed, mixer_back = jax.vjp(
        partial(mixer, segment),
        conv_in,
        head_steps.astype(jnp.float32),
        local_taps,
        local_bias,
        local_step_bias,
        local_decay,
        local_skip,
    )
    token_mixed = lax.all_to_all(
        mixed.astype(jnp.bfloat16), "seq", split_axis=0, concat_axis=1, tiled=True
    )
    normed_out, norm_back = jax.vjp(
        gate_norm, token_mixed.astype(jnp.float32), gates.astype(jnp.float32), norm_gain
    )
    normed_bf = normed_out.astype(jnp.bfloat16)
    out_whole = lax.all_gather(out_weight, "fsdp", axis=0, tiled=True)
    branch = jnp.dot(normed_bf, out_whole, preferred_element_type=jnp.float32)
    block_output = (floats + branch).astype(jnp.bfloat16)
    back_normed = lax.dot_general(
        cotangent, out_whole, contract_rows, preferred_element_type=jnp.float32
    )
    columns = normed_bf
    outward_grad = lax.psum_scatter(
        lax.dot_general(columns, cotangent, contract_tokens, preferred_element_type=jnp.float32),
        "fsdp",
        scatter_dimension=0,
        tiled=True,
    )
    back_mixed, back_gates, norm_gain_part = norm_back(back_normed)
    head_back = lax.all_to_all(
        back_mixed.astype(jnp.bfloat16), "seq", split_axis=1, concat_axis=0, tiled=True
    )
    back_conv, back_steps, taps_part, bias_part, step_part, decay_part, skip_part = mixer_back(
        head_back.astype(jnp.float32)
    )
    back_values, back_step_tokens = (
        lax.all_to_all(
            back_conv[:, :local_width].astype(jnp.bfloat16),
            "seq",
            split_axis=0,
            concat_axis=1,
            tiled=True,
        ),
        lax.all_to_all(
            back_steps.astype(jnp.bfloat16), "seq", split_axis=0, concat_axis=1, tiled=True
        ),
    )
    back_state = lax.psum_scatter(
        back_conv[:, local_width:].astype(jnp.bfloat16), "seq", scatter_dimension=0, tiled=True
    )
    back_projected = jnp.concatenate(
        [back_gates.astype(jnp.bfloat16), back_values, back_state, back_step_tokens], axis=1
    )
    back_normed_in = lax.dot_general(
        back_projected, in_whole, contract_rows, preferred_element_type=jnp.float32
    )
    columns = normed_in
    inward_grad = lax.psum_scatter(
        lax.dot_general(
            columns, back_projected, contract_tokens, preferred_element_type=jnp.float32
        ),
        "fsdp",
        scatter_dimension=0,
        tiled=True,
    )
    inward_grad, outward_grad = lax.psum((inward_grad, outward_grad), "seq")
    _, pre_back = jax.vjp(pre_norm, floats, pre_gain)
    back_floats, pre_gain_part = pre_back(back_normed_in)
    tokens_grad = cotangent.astype(jnp.float32) + back_floats
    taps_full = lax.dynamic_update_slice_in_dim(
        jnp.zeros_like(kernel_taps), taps_part[:, :local_width], head_start, 1
    )
    taps_full = taps_full.at[:, INNER:].set(taps_part[:, local_width:])
    bias_full = lax.dynamic_update_slice_in_dim(
        jnp.zeros_like(kernel_bias), bias_part[:local_width], head_start, 0
    )
    bias_full = bias_full.at[INNER:].set(bias_part[local_width:])
    step_full = lax.dynamic_update_slice_in_dim(jnp.zeros_like(step_bias), step_part, head_first, 0)
    decay_full = lax.dynamic_update_slice_in_dim(
        jnp.zeros_like(decay_log), decay_part, head_first, 0
    )
    skip_full = lax.dynamic_update_slice_in_dim(jnp.zeros_like(skip_gain), skip_part, head_first, 0)
    totals = lax.psum(
        (taps_full, bias_full, step_full, decay_full, skip_full, pre_gain_part, norm_gain_part),
        ("seq", "fsdp"),
    )
    return (
        block_output,
        tokens_grad,
        inward_grad,
        totals[0],
        totals[1],
        totals[2],
        totals[3],
        totals[4],
        totals[5],
        totals[6],
        outward_grad,
    )


def solution(mesh):
    return jax.shard_map(
        local,
        mesh=mesh,
        in_specs=(
            P(("fsdp", "seq"), None),
            P(("fsdp", "seq"), None),
            P("fsdp", None),
            P("fsdp", None),
            P(),
            P(),
            P(),
            P(),
            P(),
            P(),
            P(),
            P("fsdp", None),
        ),
        out_specs=(
            P(("fsdp", "seq"), None),
            P(("fsdp", "seq"), None),
            P("fsdp", None),
            P(),
            P(),
            P(),
            P(),
            P(),
            P(),
            P(),
            P("fsdp", None),
        ),
        check_vma=False,
    )
```

profile of v0, /device:TPU:0, one launch (start us, length us, event | category | flops | bytes accessed | tf_op | source)
XLA Modules:
  0.0 587.0 jit_solution(15330456754907170330)
XLA Ops:
  20.2 2.6 compare_convert_fusion
  24.2 68.1 %all-gather.3.cloned.1.call-done = bf16[1024,4384]{1,0:T(8,128)(2,1)} async-done(((bf16[64,4384]{1,0:T(8,128)(2,1)}), bf16[1024,4384]{1,0:T(8,128)(2,1)}) %all-gather.3.cloned.1.call-update) | async-done | bytes 8978448 | tf_op jit(solution)/shard_map/all_gather | solution.py:127
  92.3 7.3 %convolution_convert_fusion = bf16[128,4384]{0,1:T(8,128)(2,1)S(1)} fusion(bf16[1024,4384]{1,0:T(8,128)(2,1)} %all-gather.3.cloned.1.call-done, bf16[128,1024]{1,0:T(8,128)(2,1)S(1)} %copy-done.4, f32[1024]{0:T(1024)S(1)} %copy-done.23, f32[128]{0:T(128)S(1)} %fusion.99), kind=kOutput, calls=%fused_computation | convolution fusion | flops 1150324736 | bytes 10367488 | tf_op jit(solution)/shard_map/dot_general | solution.py:128
  100.3 3.2 all-to-all-start
  103.6 5.0 all_gather.10
  109.5 4.0 all-to-all-start.1
  115.8 5.5 all-to-all-done.1
  125.5 2.9 multiply_reduce_fusion.5
  133.2 6.2 %fusion.27 = f32[256,16,64]{0,2,1:T(8,128)} fusion(f32[256,256]{1,0:T(8,128)S(1)} %fusion.73, f32[16,256]{1,0:T(8,128)S(1)} %copy-done.44, pred[256,256]{1,0:T(8,128)(4,1)S(1)} %copy-done.47, f32[256,16,64]{0,2,1:T(8,128)S(1)} %bitcast.205, f32[256,16,64]{0,2,1:T(8,128)S(1)} %bitcast.193, f32[256,16]{0,1:T(8,128)S(1)} %get-tuple-element.355, ...), kind=kOutput, calls=%fused_computation.29 | convolution fusion | flops 810287104 | bytes 3522560 | tf_op jit(solution)/shard_map/jvp()/while/body/eval_jaxpr/hij,jhp->ihp/dot_general | solution.py:40
  144.6 9.3 %all_to_all.93 = bf16[2,128,1024]{1,2,0:T(8,128)(2,1)S(1)} all-to-all(bf16[2,128,1024]{1,2,0:T(8,128)(2,1)S(1)} %copy.127), channel_id=1, replica_groups=mesh['seq'=2,'fsdp'=16] {'seq'}, dimensions={0} | all-to-all | bytes 1048576 | tf_op jit(solution)/shard_map/all_to_all | solution.py:165
  157.1 4.2 multiply_reduce_fusion.6
  161.4 2.8 fusion.41
  164.2 4.2 all-to-all-start.3
  170.4 2.7 mul.647
  173.1 3.2 convolution_bitcast_fusion
  181.0 5.8 fusion.7
  186.8 4.8 fusion.34
  191.6 2.7 copy.132
  198.1 3.2 convolution_bitcast_fusion.1
  209.9 4.6 fusion.110
  215.5 2.5 reduce-window.28
  219.0 3.2 all-to-all-start.5
  223.3 2.7 all-to-all-done.5
  226.0 3.5 all-to-all-start.4
  230.6 5.5 all-to-all-done.4
  236.1 9.3 %fusion.68 = f32[1024,4384]{1,0:T(8,128)} fusion(bf16[128,32]{0,1:T(8,128)(2,1)S(1)} %bitcast.211, bf16[128,256]{0,1:T(8,128)(2,1)S(1)} %copy.149, bf16[128,2048]{0,1:T(8,128)(2,1)S(1)} %bitcast.199, bf16[128,2048]{0,1:T(8,128)(2,1)S(1)} %copy-done.13, bf16[128,1024]{1,0:T(8,128)(2,1)S(1)} %copy-done.5, f32[1024]{0:T(1024)S(1)} %copy-done.24, ...), kind=kOutput, calls=%fused_computation.108 | convolution fusion | flops 1154252800 | bytes 19345920 | tf_op jit(solution)/shard_map/dot_general | solution.py:215
  245.5 4.2 fusion.33
  253.7 73.2 %reduce-scatter.8.cloned.1.call-done = f32[128,1024]{1,0:T(8,128)} async-done(((f32[2048,1024]{1,0:T(8,128)}), f32[128,1024]{1,0:T(8,128)}) %reduce-scatter.8.cloned.1.call-update) | async-done | bytes 524304 | tf_op jit(solution)/shard_map/reduce_scatter | solution.py:179
  326.9 193.4 %reduce-scatter.6.cloned.1.call-done = f32[64,4384]{1,0:T(8,128)} async-done(((f32[1024,4384]{1,0:T(8,128)}), f32[64,4384]{1,0:T(8,128)}) %reduce-scatter.6.cloned.1.call-update) | async-done | bytes 1122320 | tf_op jit(solution)/shard_map/reduce_scatter | solution.py:214
  521.5 6.8 %fusion.51 = (f32[1024]{0:T(1024)S(1)}, f32[128]{0:T(128)S(1)}, f32[128,1024]{1,0:T(8,128)S(1)}) fusion(bf16[128,1024]{1,0:T(8,128)(2,1)S(1)} %copy-done.5, f32[128]{0:T(128)S(1)} %copy-done.59, f32[1024]{0:T(1024)S(1)} %copy-done.24, bf16[1024,4384]{1,0:T(8,128)(2,1)} %all-gather.3.cloned.1.call-done, bf16[128,32]{0,1:T(8,128)(2,1)S(1)} %bitcast.212, ...), kind=kOutput, calls=%fused_computation.90 | convolution fusion | flops 1154644864 | bytes 10896384 | tf_op jit(solution)/shard_map/dot_general | solution.py:210
  528.3 41.8 %all-reduce.16 = (f32[4,2304]{1,0:T(4,128)}, f32[2304]{0:T(1024)}, f32[32]{0:T(128)}, f32[32]{0:T(128)}, f32[32]{0:T(128)}, /*index=5*/f32[1024]{0:T(1024)}, f32[2048]{0:T(1024)}) all-reduce(f32[4,2304]{1,0:T(4,128)S(1)} %add_dynamic-update-slice_fusion, ...), channel_id=1, replica_groups=mesh['seq'=2,'fsdp'=16] {'seq','fsdp'}, use_global_device_ids=true, to_apply=%region_21.22 | all-reduce | flops 14688 | bytes 117504 | tf_op jit(solution)/shard_map/psum | solution.py:239
  571.2 5.5 all-reduce.20.cloned.1.call-done
  (288 shorter events, 67.4 us)
Async XLA Ops:
  7.2 85.1 %copy-start.4 = (bf16[128,1024]{1,0:T(8,128)(2,1)S(1)}, bf16[128,1024]{1,0:T(8,128)(2,1)}, u32[]{:S(2)}) copy-start(bf16[128,1024]{1,0:T(8,128)(2,1)} %param.16) | copy-start | bytes 786436
  7.2 85.1 %copy-start.23 = (f32[1024]{0:T(1024)S(1)}, f32[1024]{0:T(1024)}, u32[]{:S(2)}) copy-start(f32[1024]{0:T(1024)} %param.25) | copy-start | bytes 12292
  7.2 85.1 %all-gather.3.cloned.1.call-start = ((), (), s32[]{:S(2)}) async-start(), calls=%async_computation.9 | async-start | bytes 9748480 | tf_op jit(solution)/shard_map/all_gather | solution.py:127
  7.9 149.2 %all-gather.5.cloned.1.call-start = ((), (), s32[]{:S(2)}) async-start(), calls=%async_computation.10 | async-start | bytes 4456448 | tf_op jit(solution)/shard_map/all_gather | solution.py:172
  11.6 102.0 %copy-start.74 = (f32[16]{0:T(128)}, f32[16]{0:T(128)S(1)}, u32[]{:S(2)}) copy-start(f32[16]{0:T(128)S(1)} %dynamic_slice.89) | copy-start | bytes 196
  14.3 107.4 %copy-start.31 = (f32[1280]{0:T(1024)}, f32[1280]{0:T(1024)S(1)}, u32[]{:S(2)}) copy-start(f32[1280]{0:T(1024)S(1)} %get-tuple-element.316) | copy-start | bytes 15364
  14.3 107.4 %copy-start.33 = (f32[1280]{0:T(1024)}, f32[1280]{0:T(1024)S(1)}, u32[]{:S(2)}) copy-start(f32[1280]{0:T(1024)S(1)} %get-tuple-element.318) | copy-start | bytes 15364
  14.3 107.4 %copy-start.35 = (f32[1280]{0:T(1024)}, f32[1280]{0:T(1024)S(1)}, u32[]{:S(2)}) copy-start(f32[1280]{0:T(1024)S(1)} %get-tuple-element.319) | copy-start | bytes 15364
  14.3 107.4 %copy-start.37 = (f32[1280]{0:T(1024)}, f32[1280]{0:T(1024)S(1)}, u32[]{:S(2)}) copy-start(f32[1280]{0:T(1024)S(1)} %get-tuple-element.317) | copy-start | bytes 15364
  15.1 98.5 %copy-start.76 = (f32[16]{0:T(128)}, f32[16]{0:T(128)S(1)}, u32[]{:S(2)}) copy-start(f32[16]{0:T(128)S(1)} %fusion.100) | copy-start | bytes 196
  16.0 105.8 %copy-start.72 = (f32[256]{0:T(256)}, f32[256]{0:T(256)S(1)}, u32[]{:S(2)}) copy-start(f32[256]{0:T(256)S(1)} %pad_convert_fusion.1) | copy-start | bytes 3076
  17.8 104.0 %copy-start.66 = (f32[256]{0:T(256)}, f32[256]{0:T(256)S(1)}, u32[]{:S(2)}) copy-start(f32[256]{0:T(256)S(1)} %get-tuple-element.364) | copy-start | bytes 3076
  17.8 104.0 %copy-start.68 = (f32[256]{0:T(256)}, f32[256]{0:T(256)S(1)}, u32[]{:S(2)}) copy-start(f32[256]{0:T(256)S(1)} %get-tuple-element.365) | copy-start | bytes 3076
  20.2 79.5 %copy-start.79 = (f32[128]{0:T(128)}, f32[128]{0:T(128)S(1)}, u32[]{:S(2)}) copy-start(f32[128]{0:T(128)S(1)} %fusion.53) | copy-start | bytes 1540
  20.2 79.4 %copy-start.58 = (f32[128]{0:T(128)}, f32[128]{0:T(128)S(1)}, u32[]{:S(2)}) copy-start(f32[128]{0:T(128)S(1)} %fusion.99) | copy-start | bytes 1540
  100.3 9.2 %all-to-all-start = ((bf16[128,2,16]{0,2,1:T(8,128)(2,1)}), bf16[128,2,16]{0,2,1:T(8,128)(2,1)S(1)}, u32[]{:S(2)}, u32[]{:S(2)}) async-start(bf16[128,2,16]{0,2,1:T(8,128)(2,1)} %bitcast.3), calls=%async_computation | async-start | bytes 16384 | tf_op jit(solution)/shard_map/all_to_all | solution.py:137
  109.5 11.9 %all-to-all-start.1 = ((bf16[128,2,1024]{0,2,1:T(8,128)(2,1)}), bf16[128,2,1024]{0,2,1:T(8,128)(2,1)S(1)}, u32[]{:S(2)}, u32[]{:S(2)}) async-start(bf16[128,2,1024]{0,2,1:T(8,128)(2,1)} %bitcast.6), calls=%async_computation.1 | async-start | bytes 1048576 | tf_op jit(solution)/shard_map/all_to_all | solution.py:136
  164.2 12.1 %all-to-all-start.3 = ((bf16[128,2,1024]{0,2,1:T(8,128)(2,1)}), bf16[128,2,1024]{0,2,1:T(8,128)(2,1)}, u32[]{:S(2)}, u32[]{:S(2)}) async-start(bf16[128,2,1024]{0,2,1:T(8,128)(2,1)} %bitcast.201), calls=%async_computation.3 | async-start | bytes 1048576 | tf_op jit(solution)/shard_map/all_to_all | solution.py:186
  168.4 61.2 %reduce-scatter.10.cloned.1.call-start = ((), (), s32[]{:S(2)}) async-start(), calls=%async_computation.13 | async-start | bytes 196608
  209.9 117.0 %reduce-scatter.8.cloned.1.call-start = ((), (), s32[]{:S(2)}) async-start(), calls=%async_computation.12 | async-start | bytes 8912896 | tf_op jit(solution)/shard_map/reduce_scatter | solution.py:179
  219.0 7.0 %all-to-all-start.5 = ((bf16[2,128,16]{1,2,0:T(8,128)(2,1)}), bf16[2,128,16]{1,2,0:T(8,128)(2,1)S(1)}, u32[]{:S(2)}, u32[]{:S(2)}) async-start(bf16[2,128,16]{1,2,0:T(8,128)(2,1)} %copy_bitcast_fusion.3), calls=%async_computation.5 | async-start | bytes 16384 | tf_op jit(solution)/shard_map/all_to_all | solution.py:200
  222.3 13.8 %copy-start.5 = (bf16[128,1024]{1,0:T(8,128)(2,1)S(1)}, bf16[128,1024]{1,0:T(8,128)(2,1)}, u32[]{:S(2)}) copy-start(bf16[128,1024]{1,0:T(8,128)(2,1)} %param.16) | copy-start | bytes 786436
  222.3 13.8 %copy-start.13 = (bf16[128,2048]{0,1:T(8,128)(2,1)S(1)}, bf16[128,2048]{0,1:T(8,128)(2,1)}, u32[]{:S(2)}) copy-start(bf16[128,2048]{0,1:T(8,128)(2,1)} %get-tuple-element.342) | copy-start | bytes 1572868
  222.3 13.8 %copy-start.24 = (f32[1024]{0:T(1024)S(1)}, f32[1024]{0:T(1024)}, u32[]{:S(2)}) copy-start(f32[1024]{0:T(1024)} %param.25) | copy-start | bytes 12292
  222.3 13.8 %copy-start.59 = (f32[128]{0:T(128)S(1)}, f32[128]{0:T(128)}, u32[]{:S(2)}) copy-start(f32[128]{0:T(128)} %copy-done.58) | copy-start | bytes 1540
  226.0 10.1 %all-to-all-start.4 = ((bf16[2,128,1024]{1,2,0:T(8,128)(2,1)}), bf16[2,128,1024]{1,2,0:T(8,128)(2,1)S(1)}, u32[]{:S(2)}, u32[]{:S(2)}) async-start(bf16[2,128,1024]{1,2,0:T(8,128)(2,1)} %copy.133), calls=%async_computation.4 | async-start | bytes 1048576 | tf_op jit(solution)/shard_map/all_to_all | solution.py:193
  229.5 290.8 %reduce-scatter.6.cloned.1.call-start = ((), (), s32[]{:S(2)}) async-start(), calls=%async_computation.11 | async-start | bytes 19496960 | tf_op jit(solution)/shard_map/reduce_scatter | solution.py:214
  245.4 331.2 %all-reduce.20.cloned.1.call-start = ((), (), s32[]{:S(2)}) async-start(), calls=%async_computation.14 | async-start | bytes 3342336 | tf_op jit(solution)/shard_map/psum | solution.py:222
  253.6 266.7 %copy-start.49 = (f32[1280]{0:T(1024)S(1)}, f32[1280]{0:T(1024)}, u32[]{:S(2)}) copy-start(f32[1280]{0:T(1024)} %get-tuple-element.312) | copy-start | bytes 15364
  253.7 267.7 %copy-start.85 = (f32[32]{0:T(128)S(1)}, f32[32]{0:T(128)}, u32[]{:S(2)}) copy-start(f32[32]{0:T(128)} %param.23) | copy-start | bytes 388
  253.7 267.8 %copy-start.15 = (bf16[2,128,1024]{1,2,0:T(8,128)(2,1)S(1)}, bf16[2,128,1024]{1,2,0:T(8,128)(2,1)}, u32[]{:S(2)}) copy-start(bf16[2,128,1024]{1,2,0:T(8,128)(2,1)} %copy-done.14) | copy-start | bytes 1572868
  521.5 48.7 %copy-start.80 = (f32[128]{0:T(128)S(1)}, f32[128]{0:T(128)}, u32[]{:S(2)}) copy-start(f32[128]{0:T(128)} %copy-done.79) | copy-start | bytes 1540
  (65 other events, 235.8 us)
Sparse Core Ops, SparseCore 0:
  10.3 81.9 all-gather.2
  94.5 48.9 all-gather.4
  210.0 9.5 reduce-scatter.9
  223.4 103.4 reduce-scatter.7
  331.0 189.2 reduce-scatter.5
  522.5 54.1 all-reduce.19
where the time goes:
time: 593 us; the launch traced here: 587 us
  waiting for transfers between devices  355 us (60%)
  matrix products  68.9 us (12%)
  blocking collectives  56.2 us (9%)
  local copies, waits for them, and re-layouts  41.7 us (7%)
  other arithmetic  30.7 us (5%)
  starting transfers between devices  18.6 us (3%)
  between operations  15.5 us (3%)
    reduce_scatter x1, waiting for transfers between devices, local(): lax.psum_scatter(lax.dot_general(columns, back_projected, contract_tokens...  193 us
    reduce_scatter x1, waiting for transfers between devices, local(): lax.psum_scatter(lax.dot_general(columns, cotangent, contract_tokens, pre...  73.2 us
    all_gather x1, waiting for transfers between devices, local(): in_whole = lax.all_gather(in_weight, 'fsdp', axis=0, tiled=True)  68.1 us
    psum x1, blocking collectives, local(): lax.psum((taps_full, bias_full, step_full, decay_full, skip_full, pre_gai...  41.8 us
    dot_general x3, matrix products, block_step(): jnp.einsum('hij,jhp->ihp', decay * scores[None], scaled, precision=lax.Pr...  16.8 us
  transfers between devices with their start and end apart: 11, of which 7 were waited for; matrix products, arithmetic and copies ran while one was open for 16% of the time, Pallas kernels for 0%

commit v1 on v0

v1 whole, which is shorter than its diff:
```python
import jax
import jax.numpy as jnp
from jax import lax
from jax.sharding import PartitionSpec as P

HEAD_DIM = 64
STATE = 128
CONV = 4
SPAN = 256

norm_epsilon = 1e-05
bf16 = jnp.bfloat16
f32 = jnp.float32
contract_rows = (((1,), (1,)), ((), ()))
contract_tokens = (((0,), (0,)), ((), ()))


def dot(left, right, dims=(((1,), (0,)), ((), ()))):
    return lax.dot_general(left, right, dims, preferred_element_type=f32)


def pre_norm(values, gain):
    scale = lax.rsqrt(jnp.mean(values * values, axis=-1, keepdims=True) + norm_epsilon)
    return values * scale * gain


def product(spec, left, right):
    return jnp.einsum(spec, left.astype(bf16), right.astype(bf16), preferred_element_type=f32)


def mixer(segment, conv_in, step_raw, taps, tap_bias, bias_steps, log_rates, skips):
    length, channels = conv_in.shape
    heads = step_raw.shape[1]
    width = heads * HEAD_DIM
    summed = tap_bias + conv_in * taps[CONV - 1]
    for offset in range(1, CONV):
        shifted = jnp.concatenate(
            [jnp.zeros((offset, channels), f32), conv_in[: length - offset]], axis=0
        )
        matched = jnp.concatenate(
            [
                jnp.zeros((offset,), f32),
                (segment[offset:] == segment[: length - offset]).astype(f32),
            ]
        )
        summed = summed + taps[CONV - 1 - offset] * shifted * matched[:, None]
    active = jax.nn.silu(summed)
    values = active[:, :width].reshape(length, heads, HEAD_DIM).transpose(1, 0, 2)
    input_matrix = active[:, width : width + STATE]
    output_matrix = active[:, width + STATE :]
    steps_taken = jax.nn.softplus(step_raw + bias_steps)
    log_decay = (steps_taken * -jnp.exp(log_rates)).T
    scaled = values * steps_taken.T[:, :, None]
    span = min(SPAN, length)
    blocks = length // span
    places = jnp.arange(span)
    state = None
    outputs = []
    for block in range(blocks):
        at = slice(block * span, (block + 1) * span)
        seg = segment[at]
        cumul = jnp.cumsum(log_decay[:, at], axis=1)
        causal = (places[:, None] >= places[None, :]) & (seg[:, None] == seg[None, :])
        log_gap = cumul[:, :, None] - cumul[:, None, :]
        decay = jnp.where(causal[None], jnp.exp(jnp.where(causal[None], log_gap, 0.0)), 0.0)
        scores = product("in,jn->ij", output_matrix[at], input_matrix[at])
        inside = product("hij,hjp->hip", decay * scores[None], scaled[:, at])
        if state is not None:
            previous = segment[block * span - 1]
            entering = jnp.exp(cumul) * (seg == previous).astype(f32)[None]
            inside = inside + product("in,hnp->hip", output_matrix[at], state) * entering[:, :, None]
        if block + 1 < blocks:
            final = cumul[:, -1]
            leaving = jnp.exp(final[:, None] - cumul) * (seg == seg[-1]).astype(f32)[None]
            fresh = product("jn,hjp->hnp", input_matrix[at], scaled[:, at] * leaving[:, :, None])
            if state is None:
                state = fresh
            else:
                keeping = jnp.exp(final) * (seg[-1] == previous).astype(f32)
                state = keeping[:, None, None] * state + fresh
        outputs.append(inside)
    whole = outputs[0] if blocks == 1 else jnp.concatenate(outputs, axis=1)
    result = whole + values * skips[:, None, None]
    return result.transpose(1, 0, 2).reshape(length, width)


def local(
    tokens,
    cotangent,
    documents,
    in_weight,
    kernel_taps,
    kernel_bias,
    step_bias,
    decay_log,
    skip_gain,
    pre_gain,
    norm_gain,
    out_weight,
):
    groups = lax.axis_size("seq")
    shards = lax.axis_size("fsdp")
    group = lax.axis_index("seq")
    heads = step_bias.shape[0]
    inner = norm_gain.shape[0]
    states = kernel_bias.shape[0] - inner
    half = inner // groups
    spread = out_weight.shape[0] % (HEAD_DIM * groups) == 0
    parts = shards if spread else 1

    def pick(array, axis):
        size = array.shape[axis]
        lead, tail = array.shape[:axis], array.shape[axis + 1 :]
        split = array.reshape(lead + (parts, groups, size // (parts * groups)) + tail)
        chosen = lax.dynamic_index_in_dim(split, group, axis + 1, keepdims=False)
        return chosen.reshape(lead + (size // groups,) + tail)

    def place(array):
        size = array.shape[-1] * groups
        lead = array.shape[:-1]
        split = array.reshape(lead + (parts, 1, size // (parts * groups)))
        blank = jnp.zeros(lead + (parts, groups, size // (parts * groups)), array.dtype)
        full = lax.dynamic_update_slice_in_dim(blank, split, group, len(lead) + 1)
        return full.reshape(lead + (size,))

    def unite(array):
        rows, width = array.shape[1:]
        split = array.reshape(groups, rows, parts, width // parts)
        return split.transpose(1, 2, 0, 3).reshape(rows, width * groups)

    conv_end = inner + inner + states
    conv_shard = jnp.concatenate(
        [
            pick(in_weight[:, inner : 2 * inner], 1),
            in_weight[:, 2 * inner : conv_end],
            pick(in_weight[:, conv_end:], 1),
        ],
        axis=1,
    )
    conv_weight = lax.all_gather(conv_shard, "fsdp", axis=0, tiled=True)
    gate_shard, conv_weight = lax.optimization_barrier(
        (pick(in_weight[:, :inner], 1), conv_weight)
    )
    gate_weight = lax.all_gather(gate_shard, "fsdp", axis=0, tiled=True)
    out_rows = None
    if spread:
        split = out_weight.reshape(groups, out_weight.shape[0] // groups, out_weight.shape[1])
        out_rows = lax.dynamic_index_in_dim(split, group, 0, keepdims=False)
    else:
        out_rows = out_weight
    out_rows, gate_weight = lax.optimization_barrier((out_rows, gate_weight))
    out_part = lax.all_gather(out_rows, "fsdp", axis=0, tiled=True)
    if not spread:
        out_part = lax.dynamic_slice_in_dim(out_part, group * half, half, 0)

    floats = tokens.astype(f32)
    normed_own = pre_norm(floats, pre_gain).astype(bf16)
    joined = lax.all_gather(
        jnp.concatenate([normed_own, cotangent], axis=1), "seq", axis=0, tiled=True
    )
    width = tokens.shape[1]
    normed_in, cot = joined[:, :width], joined[:, width:]

    projected = dot(normed_in, conv_weight).astype(bf16).astype(f32)
    segment = documents[0]
    taps = jnp.concatenate([pick(kernel_taps[:, :inner], 1), kernel_taps[:, inner:]], axis=1)
    tap_bias = jnp.concatenate([pick(kernel_bias[:inner], 0), kernel_bias[inner:]], axis=0)
    mixed, mixer_back = jax.vjp(
        lambda *given: mixer(segment, *given),
        projected[:, : half + states],
        projected[:, half + states :],
        taps,
        tap_bias,
        pick(step_bias, 0),
        pick(decay_log, 0),
        pick(skip_gain, 0),
    )
    gain = pick(norm_gain, 0)
    gates = dot(normed_in, gate_weight).astype(bf16).astype(f32)
    mixed = mixed.astype(bf16).astype(f32)
    back_normed = dot(cot, out_part, contract_rows)
    sigmoid = jax.nn.sigmoid(gates)
    silu = gates * sigmoid
    gated = mixed * silu
    back_gain = back_normed * gain
    sums = lax.psum(
        jnp.stack([jnp.sum(gated * gated, axis=1), jnp.sum(gated * back_gain, axis=1)]), "seq"
    )
    scale = lax.rsqrt(sums[0] / inner + norm_epsilon)
    unit = gated * scale[:, None]
    normed_bf = (unit * gain).astype(bf16)
    norm_gain_part = jnp.sum(back_normed * unit, axis=0)
    back_gated = scale[:, None] * (back_gain - unit * (scale * sums[1] / inner)[:, None])
    back_mixed = (back_gated * silu).astype(bf16).astype(f32)
    back_gates = (back_gated * mixed * sigmoid * (1.0 + gates * (1.0 - sigmoid))).astype(bf16)

    outward = dot(normed_bf, cot, contract_tokens).astype(bf16)
    gate_grad = dot(normed_in, back_gates, contract_tokens).astype(bf16)
    gate_grad = lax.psum_scatter(gate_grad, "fsdp", scatter_dimension=0, tiled=True)
    if spread:
        outward = lax.psum_scatter(outward, "fsdp", scatter_dimension=0, tiled=True)
        outward_grad = lax.all_gather(outward, "seq", axis=0, tiled=True).astype(f32)
    else:
        blank = jnp.zeros((inner, width), bf16)
        outward = lax.dynamic_update_slice_in_dim(blank, outward, group * half, 0)
        outward = lax.psum_scatter(outward, "fsdp", scatter_dimension=0, tiled=True)
        outward_grad = lax.psum(outward.astype(f32), "seq")
    branch = lax.psum_scatter(
        dot(normed_bf, out_part).astype(bf16), "seq", scatter_dimension=0, tiled=True
    )
    block_output = (floats + branch.astype(f32)).astype(bf16)

    back_conv, back_steps, taps_part, bias_part, step_part, decay_part, skip_part = mixer_back(
        back_mixed
    )
    back_projected = jnp.concatenate([back_conv, back_steps], axis=1).astype(bf16)
    conv_grad = lax.psum_scatter(
        dot(normed_in, back_projected, contract_tokens).astype(bf16),
        "fsdp",
        scatter_dimension=0,
        tiled=True,
    )
    back_in = dot(back_projected, conv_weight, contract_rows) + dot(
        back_gates, gate_weight, contract_rows
    )
    back_in = lax.psum_scatter(back_in.astype(bf16), "seq", scatter_dimension=0, tiled=True)
    _, pre_back = jax.vjp(pre_norm, floats, pre_gain)
    back_floats, pre_gain_part = pre_back(back_in.astype(f32))
    tokens_grad = cotangent.astype(f32) + back_floats

    gate_all = lax.all_gather(gate_grad, "seq", axis=0).astype(f32)
    conv_all = lax.all_gather(conv_grad, "seq", axis=0).astype(f32)
    inward_grad = jnp.concatenate(
        [
            unite(gate_all),
            unite(conv_all[:, :, :half]),
            jnp.sum(conv_all[:, :, half : half + states], axis=0),
            unite(conv_all[:, :, half + states :]),
        ],
        axis=1,
    )

    pieces = (
        jnp.concatenate([place(taps_part[:, :half]), taps_part[:, half:]], axis=1),
        jnp.concatenate([place(bias_part[:half]), bias_part[half:]], axis=0),
        place(step_part),
        place(decay_part),
        place(skip_part),
        pre_gain_part,
        place(norm_gain_part),
    )
    flat = lax.psum(jnp.concatenate([piece.reshape(-1) for piece in pieces]), ("seq", "fsdp"))
    totals = []
    start = 0
    for piece in pieces:
        totals.append(flat[start : start + piece.size].reshape(piece.shape))
        start += piece.size
    return (
        block_output,
        tokens_grad,
        inward_grad,
        totals[0],
        totals[1],
        totals[2],
        totals[3],
        totals[4],
        totals[5],
        totals[6],
        outward_grad,
    )


def solution(mesh):
    rows = P(("fsdp", "seq"), None)
    split = P("fsdp", None)
    return jax.shard_map(
        local,
        mesh=mesh,
        in_specs=(rows, rows, split, split) + (P(),) * 7 + (split,),
        out_specs=(rows, rows, split) + (P(),) * 7 + (split,),
        check_vma=False,
    )
```

time: 593 us -> 462 us (0.78)
  waiting for transfers between devices: 355 us -> 285 us
  matrix products: 68.9 us -> 33.7 us
  starting transfers between devices: 18.6 us -> 0.81 us
  local copies, waits for them, and re-layouts: 41.7 us -> 32.5 us
    reduce_scatter x2 -> x5, waiting for transfers between devices: 267 us -> 154 us  [the longest x1 60.1 us: local(): lax.psum_scatter(dot(normed_in, back_projected, contract_tokens).astype(b...]
    all_gather x2 -> x4, waiting for transfers between devices: 68.1 us -> 131 us  [the longest x1 43.7 us: local(): conv_weight = lax.all_gather(conv_shard, 'fsdp', axis=0, tiled=True)]
    dot_general x15, matrix products: 66.9 us -> 33.7 us  [the longest x9 22.8 us: dot(): return lax.dot_general(left, right, dims, preferred_element_type=f32)]
    all_to_all x5 -> x0, starting transfers between devices: 18.2 us -> none  [the longest x1 4.22 us: local(): lax.all_to_all(back_mixed.astype(jnp.bfloat16), 'seq', split_axis=1, conc...]
    all_to_all x5 -> x0, waiting for transfers between devices: 13.8 us -> none  [the longest x1 5.55 us: local(): lax.all_to_all(values_raw, 'seq', split_axis=1, concat_axis=0, tiled=True)]
    all_gather x1 -> x3, blocking collectives: 5.01 us -> 18 us  [the longest x1 6.36 us: local(): conv_all = lax.all_gather(conv_grad, 'seq', axis=0).astype(f32)]
    all_to_all x1 -> x0, blocking collectives: 9.32 us -> none  [local(): lax.all_to_all(mixed.astype(jnp.bfloat16), 'seq', split_axis=0, concat_ax...]
    mul x6 -> x1, local copies, waits for them, and re-layouts: 7.83 us -> 0.07 us  [local(): back_gain = back_normed * gain]
  transfers between devices with their start and end apart: 11 -> 9, of which waited for: 7 -> 7; matrix products, arithmetic and copies ran while one was open for 16% -> 10% of each run, Pallas kernels for 0% -> 0%
where the time goes in v1:
time: 462 us; the launch traced here: 461 us
  waiting for transfers between devices  285 us (62%)
  blocking collectives  61.9 us (13%)
  matrix products  33.7 us (7%)
  local copies, waits for them, and re-layouts  32.5 us (7%)
  other arithmetic  32 us (7%)
  between operations  15.1 us (3%)
    reduce_scatter x1, waiting for transfers between devices, local(): lax.psum_scatter(dot(normed_in, back_projected, contract_tokens).astype(b...  60.1 us
    reduce_scatter x1, waiting for transfers between devices, local(): lax.psum_scatter(gate_grad, 'fsdp', scatter_dimension=0, tiled=True)  57.8 us
    all_gather x1, waiting for transfers between devices, local(): conv_weight = lax.all_gather(conv_shard, 'fsdp', axis=0, tiled=True)  43.7 us
    all_gather x1, waiting for transfers between devices, local(): gate_weight = lax.all_gather(gate_shard, 'fsdp', axis=0, tiled=True)  40.8 us
    psum x1, blocking collectives, local(): lax.psum(jnp.concatenate([piece.reshape(-1) for piece in pieces]), ('seq'...  38.7 us
    reduce_scatter x1, waiting for transfers between devices, local(): outward = lax.psum_scatter(outward, 'fsdp', scatter_dimension=0, tiled=True)  35.6 us
    all_gather x1, waiting for transfers between devices, local(): out_part = lax.all_gather(out_rows, 'fsdp', axis=0, tiled=True)  26.8 us
    dot_general x9, matrix products, dot(): return lax.dot_general(left, right, dims, preferred_element_type=f32)  22.8 us
  transfers between devices with their start and end apart: 9, of which 7 were waited for; matrix products, arithmetic and copies ran while one was open for 10% of the time, Pallas kernels for 0%

profile of v1, /device:TPU:0, one launch (start us, length us, event | category | flops | bytes accessed | tf_op | source)
XLA Modules:
  0.0 460.7 jit_solution(4221103167941699440)
XLA Ops:
  9.8 1.7 dynamic-slice_reduce_fusion
  13.0 1.7 dynamic-slice_reduce_fusion.1
  15.5 43.7 %all-gather.9.cloned.1.call-done = bf16[1024,1296]{1,0:T(8,128)(2,1)} async-done(((bf16[64,1296]{1,0:T(8,128)(2,1)}), bf16[1024,1296]{1,0:T(8,128)(2,1)}) %all-gather.9.cloned.1.call-update) | async-done | bytes 2654224 | tf_op jit(solution)/shard_map/all_gather | solution.py:140
  61.4 40.8 %all-gather.11.cloned.1.call-done = bf16[1024,1024]{1,0:T(8,128)(2,1)} async-done(((bf16[64,1024]{1,0:T(8,128)(2,1)}), bf16[1024,1024]{1,0:T(8,128)(2,1)}) %all-gather.11.cloned.1.call-update) | async-done | bytes 2097168 | tf_op jit(solution)/shard_map/all_gather | solution.py:144
  104.5 19.8 %all-gather.7.cloned.1.call-done = bf16[256,2048]{1,0:T(8,128)(2,1)} async-done(((bf16[128,2048]{1,0:T(8,128)(2,1)}), bf16[256,2048]{1,0:T(8,128)(2,1)}) %all-gather.7.cloned.1.call-update) | async-done | bytes 1048592 | tf_op jit(solution)/shard_map/all_gather | solution.py:158
  124.3 3.2 fusion.7
  130.9 4.3 fusion.79
  136.3 1.6 fusion.15
  139.0 2.5 copy.40
  141.5 26.8 %all-gather.13.cloned.1.call-done = bf16[1024,1024]{1,0:T(8,128)(2,1)} async-done(((bf16[64,1024]{1,0:T(8,128)(2,1)}), bf16[1024,1024]{1,0:T(8,128)(2,1)}) %all-gather.13.cloned.1.call-update) | async-done | bytes 2097168 | tf_op jit(solution)/shard_map/all_gather | solution.py:152
  168.3 2.6 fusion.38
  171.0 3.1 multiply_reduce_fusion.6
  174.1 5.2 %psum.14 = f32[2,256]{1,0:T(2,128)S(1)} all-reduce(f32[2,256]{1,0:T(2,128)S(1)} %pad_maximum_fusion.9), channel_id=1, replica_groups=mesh['seq'=2,'fsdp'=16] {'seq'}, use_global_device_ids=true, to_apply=%region_5.6 | all-reduce | flops 512 | bytes 4096 | tf_op jit(solution)/shard_map/psum | solution.py:186
  179.3 3.9 multiply_convert_fusion.11
  184.5 4.1 fusion.22
  188.6 3.0 fusion.6
  193.7 1.7 fusion.84
  196.0 3.8 reduce-window.16
  204.6 2.8 multiply_reduce_fusion.3
  213.4 1.8 fusion.16
  215.3 3.3 convolution_convert_fusion.5
  219.0 2.3 convolution_convert_fusion.2
  222.4 2.1 convolution_convert_fusion.3
  225.6 2.6 convolution_convert_fusion
  232.3 38.7 %psum.15 = f32[14688]{0:T(1024)S(1)} all-reduce(f32[14688]{0:T(1024)S(1)} %concatenate.66), channel_id=1, replica_groups=mesh['seq'=2,'fsdp'=16] {'seq','fsdp'}, use_global_device_ids=true, to_apply=%region_28.29 | all-reduce | flops 14688 | bytes 117504 | tf_op jit(solution)/shard_map/psum | solution.py:252
  274.2 2.1 fusion.33
  276.3 35.6 %reduce-scatter.14.cloned.1.call-done = bf16[64,1024]{1,0:T(8,128)(2,1)} async-done(((bf16[1024,1024]{1,0:T(8,128)(2,1)}), bf16[64,1024]{1,0:T(8,128)(2,1)}) %reduce-scatter.14.cloned.1.call-update) | async-done | bytes 131088 | tf_op jit(solution)/shard_map/reduce_scatter | solution.py:201
  311.9 5.8 %all_gather.35 = bf16[128,1024]{1,0:T(8,128)(2,1)S(1)} all-gather(bf16[64,1024]{1,0:T(8,128)(2,1)} %reduce-scatter.14.cloned.1.call-done), channel_id=1, replica_groups=mesh['seq'=2,'fsdp'=16] {'seq'}, dimensions={0}, use_global_device_ids=true | all-gather | bytes 393216 | tf_op jit(solution)/shard_map/all_gather | solution.py:202
  318.6 57.8 %reduce-scatter.10.cloned.1.call-done = bf16[64,1024]{1,0:T(8,128)(2,1)} async-done(((bf16[1024,1024]{1,0:T(8,128)(2,1)}), bf16[64,1024]{1,0:T(8,128)(2,1)}) %reduce-scatter.10.cloned.1.call-update) | async-done | bytes 131088 | tf_op jit(solution)/shard_map/reduce_scatter | solution.py:199
  376.4 5.8 %all-gather = bf16[128,1024]{1,0:T(8,128)(2,1)S(1)} all-gather(bf16[64,1024]{1,0:T(8,128)(2,1)} %reduce-scatter.10.cloned.1.call-done), channel_id=2, replica_groups=mesh['seq'=2,'fsdp'=16] {'seq'}, dimensions={0}, use_global_device_ids=true | all-gather | bytes 393216 | tf_op jit(solution)/shard_map/all_gather | solution.py:231
  384.3 60.1 %reduce-scatter.12.cloned.1.call-done = bf16[64,1296]{1,0:T(8,128)(2,1)} async-done(((bf16[1024,1296]{1,0:T(8,128)(2,1)}), bf16[64,1296]{1,0:T(8,128)(2,1)}) %reduce-scatter.12.cloned.1.call-update) | async-done | bytes 165904 | tf_op jit(solution)/shard_map/reduce_scatter | solution.py:217
  444.4 6.4 %all-gather.1 = bf16[128,1296]{1,0:T(8,128)(2,1)S(1)} all-gather(bf16[64,1296]{1,0:T(8,128)(2,1)} %reduce-scatter.12.cloned.1.call-done), channel_id=3, replica_groups=mesh['seq'=2,'fsdp'=16] {'seq'}, dimensions={0}, use_global_device_ids=true | all-gather | bytes 497664 | tf_op jit(solution)/shard_map/all_gather | solution.py:232
  (302 shorter events, 44.9 us)
Async XLA Ops:
  7.2 53.5 %copy-start = (bf16[128,1024]{1,0:T(8,128)(2,1)S(1)}, bf16[128,1024]{1,0:T(8,128)(2,1)}, u32[]{:S(2)}) copy-start(bf16[128,1024]{1,0:T(8,128)(2,1)} %param.23) | copy-start | bytes 786436
  7.2 52.1 %all-gather.9.cloned.1.call-start = ((), (), s32[]{:S(2)}) async-start(), calls=%async_computation.6 | async-start | bytes 3063808 | tf_op jit(solution)/shard_map/all_gather | solution.py:140
  11.7 47.6 %copy-start.11 = (bf16[128,1024]{1,0:T(8,128)(2,1)S(1)}, bf16[128,1024]{1,0:T(8,128)(2,1)}, u32[]{:S(2)}) copy-start(bf16[128,1024]{1,0:T(8,128)(2,1)} %param.12) | copy-start | bytes 786436
  12.4 47.1 %copy-start.42 = (f32[1024]{0:T(1024)S(1)}, f32[1024]{0:T(1024)}, u32[]{:S(2)}) copy-start(f32[1024]{0:T(1024)} %param.21) | copy-start | bytes 12292
  12.4 89.7 %all-gather.11.cloned.1.call-start = ((), (), s32[]{:S(2)}) async-start(), calls=%async_computation.7 | async-start | bytes 2228224 | tf_op jit(solution)/shard_map/all_gather | solution.py:144
  12.5 47.3 %copy-start.22 = (bf16[128,1024]{1,0:T(8,128)(2,1)S(1)}, bf16[128,1024]{1,0:T(8,128)(2,1)}, u32[]{:S(2)}) copy-start(bf16[128,1024]{1,0:T(8,128)(2,1)} %param.13) | copy-start | bytes 786436
  59.3 65.0 %all-gather.7.cloned.1.call-start = ((), (), s32[]{:S(2)}) async-start(), calls=%async_computation.5 | async-start | bytes 1572864 | tf_op jit(solution)/shard_map/all_gather | solution.py:158
  59.5 43.2 %copy-start.66 = (f32[128]{0:T(128)}, f32[128]{0:T(128)S(1)}, u32[]{:S(2)}) copy-start(f32[128]{0:T(128)S(1)} %fusion.34) | copy-start | bytes 1540
  59.5 42.9 %copy-start.68 = (f32[32]{0:T(128)S(1)}, f32[32]{0:T(128)}, u32[]{:S(2)}) copy-start(f32[32]{0:T(128)} %param.19) | copy-start | bytes 388
  59.5 43.0 %copy-start.69 = (f32[32]{0:T(128)S(1)}, f32[32]{0:T(128)}, u32[]{:S(2)}) copy-start(f32[32]{0:T(128)} %param.18) | copy-start | bytes 388
  59.5 43.0 %copy-start.70 = (f32[32]{0:T(128)S(1)}, f32[32]{0:T(128)}, u32[]{:S(2)}) copy-start(f32[32]{0:T(128)} %param.20) | copy-start | bytes 388
  59.5 43.1 %copy-start.61 = (f32[128]{0:T(128)}, f32[128]{0:T(128)S(1)}, u32[]{:S(2)}) copy-start(f32[128]{0:T(128)S(1)} %fusion.68) | copy-start | bytes 1540
  59.6 43.1 %slice-start.4 = ((f32[2304]{0:T(1024)}), f32[2048]{0:T(1024)S(1)}, s32[]{:S(2)}) async-start(f32[2304]{0:T(1024)} %param.17), calls=%async_computation.18 | async-start | bytes 16384 | tf_op jit(solution)/shard_map/slice | solution.py:167
  59.6 43.3 %copy-start.55 = (f32[2048]{0:T(1024)S(1)}, f32[2048]{0:T(1024)}, u32[]{:S(2)}) copy-start(f32[2048]{0:T(1024)} %param.22) | copy-start | bytes 24580
  59.6 43.5 %slice-start.2 = ((f32[4,2304]{1,0:T(4,128)}), f32[4,2048]{1,0:T(4,128)S(1)}, s32[]{:S(2)}) async-start(f32[4,2304]{1,0:T(4,128)} %param.16), calls=%async_computation.16 | async-start | bytes 65536 | tf_op jit(solution)/shard_map/slice | solution.py:166
  59.7 44.0 %slice-start.1 = ((f32[4,2304]{1,0:T(4,128)}), f32[4,256]{1,0:T(4,128)S(1)}, s32[]{:S(2)}) async-start(f32[4,2304]{1,0:T(4,128)} %param.16), calls=%async_computation.15 | async-start | bytes 8192 | tf_op jit(solution)/shard_map/slice | solution.py:166
  59.7 44.1 %copy-start.41 = (s32[1,256]{1,0:T(1,128)S(1)}, s32[1,256]{1,0:T(1,128)}, u32[]{:S(2)}) copy-start(s32[1,256]{1,0:T(1,128)} %param.14) | copy-start | bytes 3076
  59.8 44.6 %slice-start.3 = ((f32[2304]{0:T(1024)}), f32[256]{0:T(256)S(1)}, s32[]{:S(2)}) async-start(f32[2304]{0:T(1024)} %param.17), calls=%async_computation.17 | async-start | bytes 2048 | tf_op jit(solution)/shard_map/slice | solution.py:167
  60.6 107.7 %all-gather.13.cloned.1.call-start = ((), (), s32[]{:S(2)}) async-start(), calls=%async_computation.8 | async-start | bytes 2228224 | tf_op jit(solution)/shard_map/all_gather | solution.py:152
  102.1 128.8 %reduce-scatter.8.cloned.1.call-start = ((), (), s32[]{:S(2)}) async-start(), calls=%async_computation.10 | async-start | bytes 786432 | tf_op jit(solution)/shard_map/reduce_scatter | solution.py:226
  103.1 76.3 %copy-start.45 = (f32[1024]{0:T(1024)}, f32[1024]{0:T(1024)S(1)}, u32[]{:S(2)}) copy-start(f32[1024]{0:T(1024)S(1)} %mul.396) | copy-start | bytes 12292
  103.5 32.7 %copy-start.65 = (f32[16]{0:T(128)}, f32[16]{0:T(128)S(1)}, u32[]{:S(2)}) copy-start(f32[16]{0:T(128)S(1)} %dynamic-slice_reduce_fusion.4) | copy-start | bytes 196
  103.9 27.0 %copy-start.33 = (f32[1280]{0:T(1024)}, f32[1280]{0:T(1024)S(1)}, u32[]{:S(2)}) copy-start(f32[1280]{0:T(1024)S(1)} %get-tuple-element.30) | copy-start | bytes 15364
  103.9 27.0 %copy-start.35 = (f32[1280]{0:T(1024)}, f32[1280]{0:T(1024)S(1)}, u32[]{:S(2)}) copy-start(f32[1280]{0:T(1024)S(1)} %get-tuple-element.29) | copy-start | bytes 15364
  103.9 27.0 %copy-start.37 = (f32[1280]{0:T(1024)}, f32[1280]{0:T(1024)S(1)}, u32[]{:S(2)}) copy-start(f32[1280]{0:T(1024)S(1)} %get-tuple-element.31) | copy-start | bytes 15364
  130.1 58.5 %copy-start.28 = (f32[256,16]{0,1:T(8,128)}, f32[256,16]{0,1:T(8,128)S(1)}, u32[]{:S(2)}) copy-start(f32[256,16]{0,1:T(8,128)S(1)} %get-tuple-element.42) | copy-start | bytes 49156
  215.2 58.9 %reduce-scatter.6.cloned.1.call-start = ((), (), s32[]{:S(2)}) async-start(), calls=%async_computation.9 | async-start | bytes 786432 | tf_op jit(solution)/shard_map/reduce_scatter | solution.py:208
  218.7 93.2 %reduce-scatter.14.cloned.1.call-start = ((), (), s32[]{:S(2)}) async-start(), calls=%async_computation.13 | async-start | bytes 2228224 | tf_op jit(solution)/shard_map/reduce_scatter | solution.py:201
  221.4 155.0 %reduce-scatter.10.cloned.1.call-start = ((), (), s32[]{:S(2)}) async-start(), calls=%async_computation.11 | async-start | bytes 2228224 | tf_op jit(solution)/shard_map/reduce_scatter | solution.py:199
  224.5 219.9 %reduce-scatter.12.cloned.1.call-start = ((), (), s32[]{:S(2)}) async-start(), calls=%async_computation.12 | async-start | bytes 3063808 | tf_op jit(solution)/shard_map/reduce_scatter | solution.py:217
  229.4 44.1 %copy-start.67 = (f32[128]{0:T(128)S(1)}, f32[128]{0:T(128)}, u32[]{:S(2)}) copy-start(f32[128]{0:T(128)} %copy-done.66) | copy-start | bytes 1540
  229.4 44.7 %copy-start.23 = (bf16[128,1024]{1,0:T(8,128)(2,1)S(1)}, bf16[128,1024]{1,0:T(8,128)(2,1)}, u32[]{:S(2)}) copy-start(bf16[128,1024]{1,0:T(8,128)(2,1)} %param.13) | copy-start | bytes 786436
  (54 other events, 271.4 us)
Sparse Core Ops, SparseCore 0:
  12.5 46.6 all-gather.8
  62.0 40.0 all-gather.10
  104.2 19.9 all-gather.6
  126.9 41.4 all-gather.12
  215.4 13.3 reduce-scatter.7
  231.4 14.8 reduce-scatter.5
  250.1 61.7 reduce-scatter.13
  315.6 60.7 reduce-scatter.9
  380.2 64.1 reduce-scatter.11

commit v2 on v1

--- a/solution.py
+++ b/solution.py
@@ -1,6 +1,11 @@
+import functools
+import math
+
 import jax
 import jax.numpy as jnp
 from jax import lax
+from jax.experimental import pallas as pl
+from jax.experimental.pallas import tpu as pltpu
 from jax.sharding import PartitionSpec as P
 
 HEAD_DIM = 64
@@ -83,6 +88,315 @@
     result = whole + values * skips[:, None, None]
     return result.transpose(1, 0, 2).reshape(length, width)
 
+MESH = pl.DeviceIdType.MESH
+VMEM_LIMIT = 60 * 1024 * 1024
+
+
+def factors(shards):
+    rest = shards // 2
+    mid = 1 << (int(math.log2(rest)) // 2)
+    return rest // mid, mid
+
+
+def position(top, mid):
+    me = lax.axis_index("fsdp")
+    return me, me // (2 * mid), lax.rem(me // 2, mid), lax.rem(me, 2)
+
+
+def slot_of(t, m, core, mid):
+    return (t * mid + m) * 2 + core
+
+
+def greet(groups, top, mid):
+    me, t, m, core = position(top, mid)
+    group = lax.axis_index("seq")
+    peers = [{"fsdp": slot_of(lax.rem(t + d, top), m, core, mid)} for d in range(1, top)]
+    peers += [{"fsdp": slot_of(t, lax.rem(m + e, mid), core, mid)} for e in range(1, mid)]
+    peers += [{"fsdp": slot_of(t, m, 1 - core, mid)}]
+    peers += [{"seq": lax.rem(group + k, groups)} for k in range(1, groups)]
+    barrier = pltpu.get_barrier_semaphore()
+    for peer in peers:
+        pl.semaphore_signal(barrier, inc=1, device_id=peer, device_id_type=MESH)
+    pl.semaphore_wait(barrier, len(peers))
+
+
+def remote(source, target, send, receive, device):
+    copy = pltpu.make_async_remote_copy(
+        src_ref=source,
+        dst_ref=target,
+        send_sem=send,
+        recv_sem=receive,
+        device_id=device,
+        device_id_type=MESH,
+    )
+    copy.start()
+    return copy
+
+
+def gather_kernel(groups, top, mid, count, *refs):
+    rows, shards = refs[0], refs[1 : 1 + count]
+    all_rows, wholes = refs[1 + count], refs[2 + count : 2 + 2 * count]
+    send, receive, row_send, row_receive = refs[2 + 2 * count :]
+    me, t, m, core = position(top, mid)
+    group = lax.axis_index("seq")
+    greet(groups, top, mid)
+    copies = {}
+
+    def launch(a, key, source, slot, device):
+        copies[(a,) + key] = remote(
+            source, wholes[a].at[slot], send.at[(a,) + key], receive.at[(a,) + key], device
+        )
+
+    other = {"fsdp": slot_of(t, m, 1 - core, mid)}
+    for a in range(count):
+        for d in range(1, top):
+            peer = {"fsdp": slot_of(lax.rem(t + d, top), m, core, mid)}
+            launch(a, (d, 0, 0), shards[a], me, peer)
+        for e in range(1, mid):
+            peer = {"fsdp": slot_of(t, lax.rem(m + e, mid), core, mid)}
+            launch(a, (0, e, 0), shards[a], me, peer)
+        launch(a, (0, 0, 1), shards[a], me, other)
+    for k in range(1, groups):
+        copies[("rows", k)] = remote(
+            rows,
+            all_rows.at[group],
+            row_send.at[k],
+            row_receive.at[k],
+            {"seq": lax.rem(group + k, groups)},
+        )
+    for a in range(count):
+        wholes[a][me] = shards[a][...]
+    all_rows[group] = rows[...]
+    for a in range(count):
+        for d in range(1, top):
+            copies[(a, d, 0, 0)].wait_recv()
+            slot = slot_of(lax.rem(t - d + top, top), m, core, mid)
+            for e in range(1, mid):
+                peer = {"fsdp": slot_of(t, lax.rem(m + e, mid), core, mid)}
+                launch(a, (d, e, 0), wholes[a].at[slot], slot, peer)
+            launch(a, (d, 0, 1), wholes[a].at[slot], slot, other)
+    for a in range(count):
+        for d in range(top):
+            for e in range(1, mid):
+                copies[(a, d, e, 0)].wait_recv()
+                slot = slot_of(lax.rem(t - d + top, top), lax.rem(m - e + mid, mid), core, mid)
+                launch(a, (d, e, 1), wholes[a].at[slot], slot, other)
+    for key, copy in copies.items():
+        copy.wait_send()
+        if key[0] == "rows" or key[3] == 1:
+            copy.wait_recv()
+
+
+def gather_all(groups, shards, rows, arrays):
+    top, mid = factors(shards)
+    count = len(arrays)
+    vmem = pl.BlockSpec(memory_space=pltpu.VMEM)
+    out = [jax.ShapeDtypeStruct((groups,) + rows.shape, rows.dtype)]
+    out += [jax.ShapeDtypeStruct((shards,) + array.shape, array.dtype) for array in arrays]
+    return pl.pallas_call(
+        functools.partial(gather_kernel, groups, top, mid, count),
+        out_shape=out,
+        in_specs=[vmem] * (1 + count),
+        out_specs=[vmem] * (1 + count),
+        scratch_shapes=[
+            pltpu.SemaphoreType.DMA((count, top, mid, 2)),
+            pltpu.SemaphoreType.DMA((count, top, mid, 2)),
+            pltpu.SemaphoreType.DMA((groups,)),
+            pltpu.SemaphoreType.DMA((groups,)),
+        ],
+        compiler_params=pltpu.CompilerParams(
+            collective_id=0, has_side_effects=True, vmem_limit_bytes=VMEM_LIMIT
+        ),
+    )(rows, *arrays)
+
+
+CHUNKS = 2
+
+
+def add(left, right):
+    return (left.astype(f32) + right.astype(f32)).astype(bf16)
+
+
+def scatter_kernel(groups, top, mid, count, *refs):
+    partial, flat, grads = refs[0], refs[1], refs[2 : 2 + count]
+    refs = refs[2 + count :]
+    summed, total, owned = refs[0], refs[1], refs[2 : 2 + count]
+    refs = refs[2 + count :]
+    pair = refs[:count]
+    middle = refs[count : 2 * count]
+    line = refs[2 * count : 3 * count]
+    far = refs[3 * count : 4 * count]
+    flat_pair, flat_mid, flat_top, flat_group, send, receive, flat_send, flat_receive, sum_sems = (
+        refs[4 * count :]
+    )
+    me, t, m, core = position(top, mid)
+    group = lax.axis_index("seq")
+    greet(groups, top, mid)
+    other = {"fsdp": slot_of(t, m, 1 - core, mid)}
+    to_mid = [{"fsdp": slot_of(t, lax.rem(m + e, mid), core, mid)} for e in range(mid)]
+    to_top = [{"fsdp": slot_of(lax.rem(t + d, top), m, core, mid)} for d in range(top)]
+    to_group = [{"seq": lax.rem(group + k, groups)} for k in range(groups)]
+    copies = []
+
+    def launch(source, target, index, device):
+        copy = remote(source, target, send.at[index], receive.at[index], device)
+        copies.append(copy)
+        return copy
+
+    def launch_flat(stage, buffer, own, peers):
+        started = []
+        for k in range(1, len(peers)):
+            copy = remote(
+                buffer.at[own],
+                buffer.at[own],
+                flat_send.at[stage, k],
+                flat_receive.at[stage, k],
+                peers[k],
+            )
+            started.append(copy)
+            copies.append(copy)
+        return started
+
+    def total_of(buffer, started):
+        for copy in started:
+            copy.wait_recv()
+        value = buffer[0]
+        for k in range(1, buffer.shape[0]):
+            value = value + buffer[k]
+        return value
+
+    work = [(a, r) for a in range(count) for r in range(CHUNKS)]
+    rows_of = [grads[a].shape[3] // CHUNKS for a in range(count)]
+
+    def part(a, r):
+        return pl.ds(r * rows_of[a], rows_of[a])
+
+    flat_pair[core] = flat[...]
+    stage_flat = launch_flat(0, flat_pair, core, [None, other])
+    stage = {}
+    for n, (a, r) in enumerate(work):
+        stage[n] = launch(
+            grads[a].at[:, :, 1 - core, part(a, r)], pair[a].at[:, :, part(a, r)], (n, 0), other
+        )
+    sums = []
+    for k in range(1, groups):
+        copy = remote(
+            partial.at[lax.rem(group + k, groups)],
+            summed.at[group],
+            sum_sems.at[0, k],
+            sum_sems.at[1, k],
+            to_group[k],
+        )
+        sums.append(copy)
+    summed[group] = partial[group]
+
+    stage_mid = {}
+    for n, (a, r) in enumerate(work):
+        stage[n].wait_recv()
+
+        @pl.loop(0, top)
+        def _(i):
+            for j in range(mid):
+                at = part(a, r)
+                pair[a][i, j, at] = add(pair[a][i, j, at], grads[a][i, j, core, at])
+
+        for e in range(1, mid):
+            stage_mid[n, e] = launch(
+                pair[a].at[:, lax.rem(m + e, mid), part(a, r)],
+                middle[a].at[e - 1, :, part(a, r)],
+                (n, e),
+                to_mid[e],
+            )
+        if n == 0:
+            flat_mid[m] = total_of(flat_pair, stage_flat)
+            stage_flat = launch_flat(1, flat_mid, m, to_mid)
+    stage_top = {}
+    for n, (a, r) in enumerate(work):
+        for e in range(1, mid):
+            stage_mid[n, e].wait_recv()
+
+        @pl.loop(0, top)
+        def _(i):
+            at = part(a, r)
+            value = pair[a][i, m, at].astype(f32)
+            for e in range(1, mid):
+                value = value + middle[a][e - 1, i, at].astype(f32)
+            line[a][i, at] = value.astype(bf16)
+
+        for d in range(1, top):
+            stage_top[n, d] = launch(
+                line[a].at[lax.rem(t + d, top), part(a, r)],
+                far[a].at[d - 1, part(a, r)],
+                (n, mid + d - 1),
+                to_top[d],
+            )
+        if n == 0:
+            flat_top[t] = total_of(flat_mid, stage_flat)
+            stage_flat = launch_flat(2, flat_top, t, to_top)
+    last = []
+    for n, (a, r) in enumerate(work):
+        at = part(a, r)
+        for d in range(1, top):
+            stage_top[n, d].wait_recv()
+        value = line[a][t, at].astype(f32)
+        for d in range(1, top):
+            value = value + far[a][d - 1, at].astype(f32)
+        owned[a][group, at] = value.astype(bf16)
+        for k in range(1, groups):
+            last.append(
+                launch(
+                    owned[a].at[group, at],
+                    owned[a].at[group, at],
+                    (n, mid + top - 2 + k),
+                    to_group[k],
+                )
+            )
+        if n == 0:
+            flat_group[group] = total_of(flat_top, stage_flat)
+            stage_flat = launch_flat(3, flat_group, group, to_group)
+    total[...] = total_of(flat_group, stage_flat)
+    for copy in last:
+        copy.wait_recv()
+    for copy in sums:
+        copy.wait()
+    for copy in copies:
+        copy.wait_send()
+
+
+def scatter_all(groups, shards, partial, flat, grads):
+    top, mid = factors(shards)
+    count = len(grads)
+    vmem = pl.BlockSpec(memory_space=pltpu.VMEM)
+    grads = [grad.reshape(top, mid, 2, grad.shape[0] // shards, grad.shape[1]) for grad in grads]
+    shapes = [grad.shape[3:] for grad in grads]
+    out = [
+        jax.ShapeDtypeStruct(partial.shape, bf16),
+        jax.ShapeDtypeStruct(flat.shape, f32),
+    ] + [jax.ShapeDtypeStruct((groups,) + shape, bf16) for shape in shapes]
+    most = max(2, mid, top, groups)
+    stages = mid + top + groups - 2
+    return pl.pallas_call(
+        functools.partial(scatter_kernel, groups, top, mid, count),
+        out_shape=out,
+        in_specs=[vmem] * (2 + count),
+        out_specs=[vmem] * (2 + count),
+        scratch_shapes=[pltpu.VMEM((top, mid) + shape, bf16) for shape in shapes]
+        + [pltpu.VMEM((max(1, mid - 1), top) + shape, bf16) for shape in shapes]
+        + [pltpu.VMEM((top,) + shape, bf16) for shape in shapes]
+        + [pltpu.VMEM((max(1, top - 1),) + shape, bf16) for shape in shapes]
+        + [pltpu.VMEM((size,) + flat.shape, f32) for size in (2, mid, top, groups)]
+        + [
+            pltpu.SemaphoreType.DMA((count * CHUNKS, stages)),
+            pltpu.SemaphoreType.DMA((count * CHUNKS, stages)),
+            pltpu.SemaphoreType.DMA((4, most)),
+            pltpu.SemaphoreType.DMA((4, most)),
+            pltpu.SemaphoreType.DMA((2, groups)),
+        ],
+        compiler_params=pltpu.CompilerParams(
+            collective_id=1, has_side_effects=True, vmem_limit_bytes=VMEM_LIMIT
+        ),
+    )(partial, flat, *grads)
+
 
 def local(
     tokens,
@@ -137,28 +451,26 @@
         ],
         axis=1,
     )
-    conv_weight = lax.all_gather(conv_shard, "fsdp", axis=0, tiled=True)
-    gate_shard, conv_weight = lax.optimization_barrier(
-        (pick(in_weight[:, :inner], 1), conv_weight)
-    )
-    gate_weight = lax.all_gather(gate_shard, "fsdp", axis=0, tiled=True)
-    out_rows = None
+    gate_shard = pick(in_weight[:, :inner], 1)
+    out_rows = out_weight
     if spread:
         split = out_weight.reshape(groups, out_weight.shape[0] // groups, out_weight.shape[1])
         out_rows = lax.dynamic_index_in_dim(split, group, 0, keepdims=False)
-    else:
-        out_rows = out_weight
-    out_rows, gate_weight = lax.optimization_barrier((out_rows, gate_weight))
-    out_part = lax.all_gather(out_rows, "fsdp", axis=0, tiled=True)
+    floats = tokens.astype(f32)
+    normed_own = pre_norm(floats, pre_gain).astype(bf16)
+    count, width = tokens.shape
+    joined, conv_weight, gate_weight, out_part = gather_all(
+        groups,
+        shards,
+        jnp.concatenate([normed_own, cotangent], axis=1),
+        [conv_shard, gate_shard, out_rows],
+    )
+    joined = joined.reshape(groups * count, 2 * width)
+    conv_weight = conv_weight.reshape(width, -1)
+    gate_weight = gate_weight.reshape(width, -1)
+    out_part = out_part.reshape(-1, width)
     if not spread:
         out_part = lax.dynamic_slice_in_dim(out_part, group * half, half, 0)
-
-    floats = tokens.astype(f32)
-    normed_own = pre_norm(floats, pre_gain).astype(bf16)
-    joined = lax.all_gather(
-        jnp.concatenate([normed_own, cotangent], axis=1), "seq", axis=0, tiled=True
-    )
-    width = tokens.shape[1]
     normed_in, cot = joined[:, :width], joined[:, width:]
 
     projected = dot(normed_in, conv_weight).astype(bf16).astype(f32)
@@ -196,40 +508,55 @@
 
     outward = dot(normed_bf, cot, contract_tokens).astype(bf16)
     gate_grad = dot(normed_in, back_gates, contract_tokens).astype(bf16)
-    gate_grad = lax.psum_scatter(gate_grad, "fsdp", scatter_dimension=0, tiled=True)
-    if spread:
-        outward = lax.psum_scatter(outward, "fsdp", scatter_dimension=0, tiled=True)
-        outward_grad = lax.all_gather(outward, "seq", axis=0, tiled=True).astype(f32)
-    else:
+    if not spread:
         blank = jnp.zeros((inner, width), bf16)
         outward = lax.dynamic_update_slice_in_dim(blank, outward, group * half, 0)
-        outward = lax.psum_scatter(outward, "fsdp", scatter_dimension=0, tiled=True)
-        outward_grad = lax.psum(outward.astype(f32), "seq")
-    branch = lax.psum_scatter(
-        dot(normed_bf, out_part).astype(bf16), "seq", scatter_dimension=0, tiled=True
-    )
-    block_output = (floats + branch.astype(f32)).astype(bf16)
+    branch = dot(normed_bf, out_part).astype(bf16)
 
     back_conv, back_steps, taps_part, bias_part, step_part, decay_part, skip_part = mixer_back(
         back_mixed
     )
     back_projected = jnp.concatenate([back_conv, back_steps], axis=1).astype(bf16)
-    conv_grad = lax.psum_scatter(
-        dot(normed_in, back_projected, contract_tokens).astype(bf16),
-        "fsdp",
-        scatter_dimension=0,
-        tiled=True,
-    )
+    conv_grad = dot(normed_in, back_projected, contract_tokens).astype(bf16)
     back_in = dot(back_projected, conv_weight, contract_rows) + dot(
         back_gates, gate_weight, contract_rows
     )
-    back_in = lax.psum_scatter(back_in.astype(bf16), "seq", scatter_dimension=0, tiled=True)
-    _, pre_back = jax.vjp(pre_norm, floats, pre_gain)
-    back_floats, pre_gain_part = pre_back(back_in.astype(f32))
-    tokens_grad = cotangent.astype(f32) + back_floats
-
-    gate_all = lax.all_gather(gate_grad, "seq", axis=0).astype(f32)
-    conv_all = lax.all_gather(conv_grad, "seq", axis=0).astype(f32)
+    pre_gain_part = jnp.sum(back_in * normed_in.astype(f32), axis=0) / pre_gain
+
+    pieces = (
+        jnp.concatenate([place(taps_part[:, :half]), taps_part[:, half:]], axis=1),
+        jnp.concatenate([place(bias_part[:half]), bias_part[half:]], axis=0),
+        place(step_part),
+        place(decay_part),
+        place(skip_part),
+        pre_gain_part,
+        place(norm_gain_part),
+    )
+    flat = jnp.concatenate([piece.reshape(-1) for piece in pieces])
+    padded = jnp.pad(flat, (0, -flat.size % 1024)).reshape(-1, 128)
+    partial = jnp.concatenate(
+        [
+            back_in.astype(bf16).reshape(groups, count, width),
+            branch.reshape(groups, count, width),
+        ],
+        axis=1,
+    )
+    partial, padded, conv_all, gate_all, out_all = scatter_all(
+        groups, shards, partial, padded, [conv_grad, gate_grad, outward]
+    )
+    partial = jnp.sum(partial.astype(f32), axis=0)
+    block_output = (floats + partial[count:]).astype(bf16)
+    _, pre_back = jax.vjp(lambda given: pre_norm(given, pre_gain), floats)
+    tokens_grad = cotangent.astype(f32) + pre_back(partial[:count])[0]
+    conv_all, gate_all, out_all = (
+        conv_all.astype(f32),
+        gate_all.astype(f32),
+        out_all.astype(f32),
+    )
+    if spread:
+        outward_grad = out_all.reshape(-1, width)
+    else:
+        outward_grad = jnp.sum(out_all, axis=0)
     inward_grad = jnp.concatenate(
         [
             unite(gate_all),
@@ -239,17 +566,7 @@
         ],
         axis=1,
     )
-
-    pieces = (
-        jnp.concatenate([place(taps_part[:, :half]), taps_part[:, half:]], axis=1),
-        jnp.concatenate([place(bias_part[:half]), bias_part[half:]], axis=0),
-        place(step_part),
-        place(decay_part),
-        place(skip_part),
-        pre_gain_part,
-        place(norm_gain_part),
-    )
-    flat = lax.psum(jnp.concatenate([piece.reshape(-1) for piece in pieces]), ("seq", "fsdp"))
+    flat = padded.reshape(-1)
     totals = []
     start = 0
     for piece in pieces:

time: 462 us -> 234 us (0.51)
  waiting for transfers between devices: 285 us -> 0 us
  Pallas kernels: 0 us -> 125 us
  blocking collectives: 61.9 us -> 4.98 us
  between operations: 15.1 us -> 1.59 us
    reduce_scatter x5 -> x0, waiting for transfers between devices: 154 us -> none  [the longest x1 60.1 us: local(): lax.psum_scatter(dot(normed_in, back_projected, contract_tokens).astype(b...]
    all_gather x4 -> x0, waiting for transfers between devices: 131 us -> none  [the longest x1 43.7 us: local(): conv_weight = lax.all_gather(conv_shard, 'fsdp', axis=0, tiled=True)]
    pallas_call x0 -> x2, Pallas kernels: none -> 125 us  [the longest x1 67.3 us: scatter_all(): pl.pallas_call(functools.partial(scatter_kernel, groups, top, mid, count)...]
    psum x1 -> x0, blocking collectives: 38.7 us -> none  [local(): lax.psum(jnp.concatenate([piece.reshape(-1) for piece in pieces]), ('seq'...]
    all_gather x3 -> x0, blocking collectives: 18 us -> none  [the longest x1 6.36 us: local(): conv_all = lax.all_gather(conv_grad, 'seq', axis=0).astype(f32)]
  transfers between devices with their start and end apart: 9 -> 0, of which waited for: 7 -> 0; matrix products, arithmetic and copies ran while one was open for 10% -> 0% of each run, Pallas kernels for 0% -> 0%
where the time goes in v2:
time: 234 us; the launch traced here: 233 us
  Pallas kernels  125 us (53%)
  matrix products  35.8 us (15%)
  local copies, waits for them, and re-layouts  34.4 us (15%)
  other arithmetic  31.2 us (13%)
  blocking collectives  4.98 us (2%)
    pallas_call x1, Pallas kernels, scatter_all(): pl.pallas_call(functools.partial(scatter_kernel, groups, top, mid, count)...  67.3 us
    pallas_call x1, Pallas kernels, gather_all(): pl.pallas_call(functools.partial(gather_kernel, groups, top, mid, count),...  57.4 us
    dot_general x9, matrix products, dot(): return lax.dot_general(left, right, dims, preferred_element_type=f32)  24.4 us
    dot_general x6, matrix products, product(): jnp.einsum(spec, left.astype(bf16), right.astype(bf16), preferred_element...  11.4 us
    another operation x6, other arithmetic  7.91 us
    unnamed x99, local copies, waits for them, and re-layouts  4.98 us
    psum x1, blocking collectives, local(): lax.psum(jnp.stack([jnp.sum(gated * gated, axis=1), jnp.sum(gated * back_...  4.98 us

profile of v2, /device:TPU:0, one launch (start us, length us, event | category | flops | bytes accessed | tf_op | source)
XLA Modules:
  0.0 232.7 jit_solution(1653569507043543539)
XLA Ops:
  0.7 1.2 fusion.29
  4.0 1.8 pad_maximum_fusion.3.refs_0_
  7.1 3.3 %dynamic-slice_reduce_fusion = (bf16[64,16,64]{2,1,0:T(8,128)(2,1)S(1)}, bf16[64,16,64]{2,1,0:T(8,128)(2,1)S(1)}) fusion(bf16[64,16,2,64]{3,2,1,0:T(2,128)(2,1)S(1)} %reshape.424, s32[]{:T(128)S(6)} %select_n.50, bf16[64,16,2,64]{3,2,1,0:T(2,128)(2,1)S(1)} %reshape.420), kind=kLoop, calls=%fused_computation.90 | loop fusion | bytes 524292 | tf_op jit(solution)/shard_map/jit(dynamic_index_in_dim)/dynamic_slice | solution.py:429
  12.9 57.4 %shard_map.203 = (bf16[2,128,2048]{2,1,0:T(8,128)(2,1)}, bf16[16,64,1296]{2,1,0:T(8,128)(2,1)}, bf16[16,64,1024]{2,1,0:T(8,128)(2,1)}, bf16[16,64,1024]{2,1,0:T(8,128)(2,1)}) custom-call(bf16[128,2048]{1,0:T(8,128)(2,1)} %pad_maximum_fusion.3.refs_0_, bf16[64,1296]{1,0:T(8,128)(2,1)} %pad_maximum_fusion.6.refs_1_, bf16[64,1024]{1,0:T(8,128)(2,1)} %reshape.425.refs_2_, ...), custom_call_target="tpu_custom_call" | custom-call | tf_op jit(solution)/shard_map/pallas_call | solution.py:196
  70.5 3.2 %fusion.7 = f32[256,1296]{0,1:T(8,128)S(1)} fusion(bf16[1024,1296]{1,0:T(8,128)(2,1)} %bitcast.155, bf16[256,2048]{1,0:T(8,128)(2,1)} %bitcast.141), kind=kOutput, calls=%fused_computation.13 | convolution fusion | flops 680140800 | bytes 4734976 | tf_op jit(solution)/shard_map/dot_general | solution.py:24
  75.0 1.2 slice.237
  76.2 1.2 slice.236
  77.8 4.7 %fusion.76 = (bf16[256,1280]{0,1:T(8,128)(2,1)S(1)}, f32[256,1280]{0,1:T(8,128)}, f32[256,1280]{0,1:T(8,128)}) fusion(f32[256]{0:T(256)S(1)} %get-tuple-element.83, f32[253,1280]{0,1:T(8,128)S(1)} %slice.238, f32[1280]{0:T(1024)S(1)} %get-tuple-element.36, f32[256]{0:T(256)S(1)} %pad_convert_fusion.1, f32[254,1280]{0,1:T(8,128)} %slice.237, ...), kind=kLoop, calls=%fused_computation.184 | loop fusion | flops 5242880 | bytes 8517632 | tf_op jit(solution)/shard_map/convert.23
  85.3 1.3 slice.241
  86.7 1.6 fusion.15
  89.4 2.5 %copy.43 = f32[256,1024]{1,0:T(8,128)} copy(f32[256,1024]{0,1:T(8,128)} %bitcast_convert_fusion) | data formatting | bytes 2097152 | tf_op jit(solution)/shard_map/convert_element_type | solution.py:492
  91.9 3.5 %fusion.35 = f32[256,1024]{1,0:T(8,128)} fusion(bf16[1024,1024]{1,0:T(8,128)(2,1)} %bitcast.160, bf16[256,2048]{1,0:T(8,128)(2,1)} %bitcast.142), kind=kOutput, calls=%fused_computation.93 | convolution fusion | flops 536870912 | bytes 3670016 | tf_op jit(solution)/shard_map/dot_general | solution.py:24
  95.5 3.4 %multiply_reduce_fusion.7 = (f32[256]{0:T(256)S(1)}, f32[256]{0:T(256)S(1)}, bf16[256,1024]{1,0:T(8,128)(2,1)S(1)}) fusion(f32[256,1024]{1,0:T(8,128)} %copy.43, f32[256,1024]{1,0:T(8,128)} %fusion.35, f32[1024]{0:T(1024)S(1)} %mul.392, bf16[1024,1024]{1,0:T(8,128)(2,1)} %bitcast.158, bf16[256,2048]{1,0:T(8,128)(2,1)} %bitcast.143), kind=kOutput, calls=%fused_computation.69 | convolution fusion | flops 540016128 | bytes 5249024 | tf_op jit(solution)/shard_map/dot_general | solution.py:24
  98.9 5.0 %psum.7 = f32[2,256]{1,0:T(2,128)S(1)} all-reduce(f32[2,256]{1,0:T(2,128)S(1)} %pad_maximum_fusion.10), channel_id=1, replica_groups=mesh['seq'=2,'fsdp'=16] {'seq'}, use_global_device_ids=true, to_apply=%region_5.6 | all-reduce | flops 512 | bytes 4096 | tf_op jit(solution)/shard_map/psum | solution.py:498
  103.9 3.7 %convolution_convert_fusion.5 = bf16[256,1024]{1,0:T(8,128)(2,1)} fusion(bf16[1024,1024]{1,0:T(8,128)(2,1)} %bitcast.161, f32[256]{0:T(256)S(1)} %bitcast.174, f32[1024]{0:T(1024)S(1)} %mul.392, f32[256,1024]{1,0:T(8,128)} %copy.43, bf16[256,1024]{1,0:T(8,128)(2,1)S(1)} %get-tuple-element.72), kind=kOutput, calls=%fused_computation.45 | convolution fusion | flops 539492352 | bytes 4199424 | tf_op jit(solution)/shard_map/dot_general | solution.py:24
  107.6 2.9 %multiply_convert_fusion.12 = (bf16[256,1024]{1,0:T(8,128)(2,1)}, bf16[256,1024]{1,0:T(8,128)(2,1)S(1)}, f32[1024]{0:T(1024)S(1)}) fusion(f32[256]{0:T(256)S(1)} %multiply_multiply_fusion, f32[256,1024]{1,0:T(8,128)S(1)} %copy-done.6, f32[256]{0:T(256)S(1)} %bitcast.176, f32[1024]{0:T(1024)S(1)} %mul.392, bf16[256,1024]{1,0:T(8,128)(2,1)} %copy-done.23, ...), kind=kLoop, calls=%fused_computation.66 | loop fusion | flops 5766144 | bytes 3680256 | tf_op jit(solution)/shard_map/convert_element_type | solution.py:506
  110.5 1.8 fusion.81
  112.3 2.0 copy.44
  114.3 3.8 %fusion.21 = (f32[16,256]{1,0:T(8,128)S(1)}, bf16[16,256,64]{1,2,0:T(8,128)(2,1)}) fusion(f32[256,1280]{0,1:T(8,128)} %get-tuple-element.52, bf16[16,256,64]{1,2,0:T(8,128)(2,1)} %bitcast.138, f32[256,256]{1,0:T(8,128)} %copy-done.29, f32[16,256]{1,0:T(8,128)S(1)} %copy_bitcast_fusion, pred[256,256]{1,0:T(8,128)(4,1)} %copy-done.33), kind=kOutput, calls=%fused_computation.55 | convolution fusion | flops 140505088 | bytes 2473984 | tf_op jit(solution)/shard_map/transpose(jvp(hij,hjp->hip))/dot_general | solution.py:33
  118.1 3.9 %fusion.6 = (f32[16,256]{1,0:T(8,128)S(1)}, f32[16,256]{1,0:T(8,128)S(1)}, bf16[256,256]{1,0:T(8,128)(2,1)}) fusion(f32[256,256]{1,0:T(8,128)S(1)} %copy-done.30, f32[16,256]{1,0:T(8,128)S(1)} %copy_bitcast_fusion, pred[256,256]{1,0:T(8,128)(4,1)S(1)} %copy-done.34, bf16[16,256,64]{1,2,0:T(8,128)(2,1)S(1)} %bitcast.139, f32[16,256,64]{1,2,0:T(8,128)S(1)} %bitcast.151, ...), kind=kOutput, calls=%fused_computation.11 | convolution fusion | flops 148299776 | bytes 2097152 | tf_op jit(solution)/shard_map/transpose(jvp(hij,hjp->hip))/dot_general | solution.py:33
  122.0 2.5 %reduce-window.16 = f32[16,2,128]{2,0,1:T(8,128)S(1)} reduce-window(f32[16,2,128]{2,0,1:T(8,128)S(1)} %copy_bitcast_fusion.1, f32[]{:T(128)} %constant.81.clone.1), window={size=1x1x128 pad=0_0x0_0x0_127}, to_apply=%region_10.11 | reduce-window | flops 520192 | bytes 32772 | tf_op jit(solution)/shard_map/reduce-window.2
  124.6 1.4 fusion.73
  126.0 1.6 fusion.17
  131.3 1.3 multiply_reduce_fusion.2
  135.6 1.2 copy-done.15
  142.0 2.1 convolution_convert_fusion
  144.1 3.1 %copy.51 = bf16[1024,1296]{1,0:T(8,128)(2,1)} copy(bf16[1024,1296]{0,1:T(8,128)(2,1)S(1)} %convolution_convert_fusion) | data formatting | bytes 5308416 | tf_op jit(solution)/shard_map/convert_element_type | solution.py:520
  147.2 3.3 %convolution_convert_fusion.3 = bf16[1024,1024]{1,0:T(8,128)(2,1)} fusion(bf16[256,1024]{1,0:T(8,128)(2,1)S(1)} %get-tuple-element.55, bf16[256,2048]{1,0:T(8,128)(2,1)} %bitcast.145), kind=kOutput, calls=%fused_computation.19 | convolution fusion | flops 537919488 | bytes 3145728 | tf_op jit(solution)/shard_map/dot_general | solution.py:24
  150.5 2.4 %convolution_convert_fusion.2 = bf16[1024,1024]{1,0:T(8,128)(2,1)} fusion(bf16[256,2048]{1,0:T(8,128)(2,1)S(1)} %bitcast.147, f32[256]{0:T(256)S(1)} %bitcast.177, f32[1024]{0:T(1024)S(1)} %mul.392, f32[256,1024]{1,0:T(8,128)S(1)} %copy-done.10, bf16[256,1024]{1,0:T(8,128)(2,1)S(1)} %copy-done.24), kind=kOutput, calls=%fused_computation.18 | convolution fusion | flops 540278784 | bytes 4199424 | tf_op jit(solution)/shard_map/dot_general | solution.py:24
  152.8 67.3 %shard_map.204 = (bf16[2,256,1024]{2,1,0:T(8,128)(2,1)}, f32[120,128]{1,0:T(8,128)}, bf16[2,64,1296]{2,1,0:T(8,128)(2,1)}, bf16[2,64,1024]{2,1,0:T(8,128)(2,1)}, bf16[2,64,1024]{2,1,0:T(8,128)(2,1)}) custom-call(bf16[2,256,1024]{2,1,0:T(8,128)(2,1)} %pad_maximum_fusion.1.refs_0_, f32[120,128]{1,0:T(8,128)} %pad_bitcast_fusion.refs_1_, ...), custom_call_target="tpu_custom_call" | custom-call | tf_op jit(solution)/shard_map/pallas_call | solution.py:378
  220.2 1.6 convert_reduce_fusion
  222.0 1.1 fusion.28
  (232 shorter events, 33.1 us)
Async XLA Ops:
  0.6 11.5 %copy-start = (bf16[128,1024]{1,0:T(8,128)(2,1)S(1)}, bf16[128,1024]{1,0:T(8,128)(2,1)}, u32[]{:S(2)}) copy-start(bf16[128,1024]{1,0:T(8,128)(2,1)} %param.23) | copy-start | bytes 786436
  0.7 5.1 %slice-start = ((bf16[64,4384]{1,0:T(8,128)(2,1)}), bf16[64,32]{1,0:T(8,128)(2,1)S(1)}, s32[]{:S(2)}) async-start(bf16[64,4384]{1,0:T(8,128)(2,1)} %param.15), calls=%async_computation | async-start | bytes 32768 | tf_op jit(solution)/shard_map/slice | solution.py:450
  0.7 5.3 %copy-start.22 = (bf16[64,4384]{1,0:T(8,128)(2,1)S(1)}, bf16[64,4384]{1,0:T(8,128)(2,1)}, u32[]{:S(2)}) copy-start(bf16[64,4384]{1,0:T(8,128)(2,1)} %param.15) | copy-start | bytes 1683460
  6.5 4.1 %slice-start.1 = ((bf16[64,4384]{1,0:T(8,128)(2,1)}), bf16[64,256]{1,0:T(8,128)(2,1)S(1)}, s32[]{:S(2)}) async-start(bf16[64,4384]{1,0:T(8,128)(2,1)} %param.15), calls=%async_computation.1 | async-start | bytes 65536 | tf_op jit(solution)/shard_map/slice | solution.py:449
  10.4 59.8 %copy-start.32 = (s32[1,256]{1,0:T(1,128)S(1)}, s32[1,256]{1,0:T(1,128)}, u32[]{:S(2)}) copy-start(s32[1,256]{1,0:T(1,128)} %param.14) | copy-start | bytes 3076
  75.0 2.7 %copy-start.38 = (f32[256]{0:T(256)}, f32[256]{0:T(256)S(1)}, u32[]{:S(2)}) copy-start(f32[256]{0:T(256)S(1)} %pad_convert_fusion.1) | copy-start | bytes 3076
  77.7 5.8 %copy-start.46 = (f32[32]{0:T(128)S(1)}, f32[32]{0:T(128)}, u32[]{:S(2)}) copy-start(f32[32]{0:T(128)} %param.20) | copy-start | bytes 388
  77.8 5.9 %copy-start.47 = (f32[32]{0:T(128)S(1)}, f32[32]{0:T(128)}, u32[]{:S(2)}) copy-start(f32[32]{0:T(128)} %param.19) | copy-start | bytes 388
  77.8 6.2 %copy-start.48 = (f32[32]{0:T(128)S(1)}, f32[32]{0:T(128)}, u32[]{:S(2)}) copy-start(f32[32]{0:T(128)} %param.18) | copy-start | bytes 388
  83.5 4.7 %copy-start.29 = (f32[256,256]{1,0:T(8,128)}, f32[256,256]{1,0:T(8,128)S(1)}, u32[]{:S(2)}) copy-start(f32[256,256]{1,0:T(8,128)S(1)} %fusion.44) | copy-start | bytes 786436
  83.9 4.3 %copy-start.42 = (f32[16]{0:T(128)}, f32[16]{0:T(128)S(1)}, u32[]{:S(2)}) copy-start(f32[16]{0:T(128)S(1)} %get-tuple-element.80) | copy-start | bytes 196
  84.2 4.0 %copy-start.37 = (f32[16]{0:T(128)}, f32[16]{0:T(128)S(1)}, u32[]{:S(2)}) copy-start(f32[16]{0:T(128)S(1)} %dynamic-slice_reduce_fusion.6) | copy-start | bytes 196
  85.3 3.0 %copy-start.33 = (pred[256,256]{1,0:T(8,128)(4,1)}, pred[256,256]{1,0:T(8,128)(4,1)S(1)}, u32[]{:S(2)}) copy-start(pred[256,256]{1,0:T(8,128)(4,1)S(1)} %fusion.42) | copy-start | bytes 196612
  98.9 8.7 %copy-start.23 = (bf16[256,1024]{1,0:T(8,128)(2,1)}, bf16[256,1024]{1,0:T(8,128)(2,1)S(1)}, u32[]{:S(2)}) copy-start(bf16[256,1024]{1,0:T(8,128)(2,1)S(1)} %get-tuple-element.72) | copy-start | bytes 1572868
  103.9 3.7 %copy-start.6 = (f32[256,1024]{1,0:T(8,128)S(1)}, f32[256,1024]{1,0:T(8,128)}, u32[]{:S(2)}) copy-start(f32[256,1024]{1,0:T(8,128)} %fusion.35) | copy-start | bytes 3145732
  103.9 3.7 %copy-start.9 = (f32[256,1024]{1,0:T(8,128)S(1)}, f32[256,1024]{1,0:T(8,128)}, u32[]{:S(2)}) copy-start(f32[256,1024]{1,0:T(8,128)} %copy.43) | copy-start | bytes 3145732
  107.6 2.9 %copy-start.18 = (bf16[16,64,1024]{2,1,0:T(8,128)(2,1)S(1)}, bf16[16,64,1024]{2,1,0:T(8,128)(2,1)}, u32[]{:S(2)}) copy-start(bf16[16,64,1024]{2,1,0:T(8,128)(2,1)} %get-tuple-element.22) | copy-start | bytes 6291460
  114.3 3.8 %copy-start.4 = (bf16[256,1024]{0,1:T(8,128)(2,1)S(1)}, bf16[256,1024]{0,1:T(8,128)(2,1)}, u32[]{:S(2)}) copy-start(bf16[256,1024]{0,1:T(8,128)(2,1)} %copy.44) | copy-start | bytes 1572868
  114.3 3.8 %copy-start.12 = (f32[256,1024]{0,1:T(8,128)S(1)}, f32[256,1024]{0,1:T(8,128)}, u32[]{:S(2)}) copy-start(f32[256,1024]{0,1:T(8,128)} %copy-done.11) | copy-start | bytes 3145732
  114.3 3.8 %copy-start.30 = (f32[256,256]{1,0:T(8,128)S(1)}, f32[256,256]{1,0:T(8,128)}, u32[]{:S(2)}) copy-start(f32[256,256]{1,0:T(8,128)} %copy-done.29) | copy-start | bytes 786436
  114.3 3.8 %copy-start.34 = (pred[256,256]{1,0:T(8,128)(4,1)S(1)}, pred[256,256]{1,0:T(8,128)(4,1)}, u32[]{:S(2)}) copy-start(pred[256,256]{1,0:T(8,128)(4,1)} %copy-done.33) | copy-start | bytes 196612
  124.6 3.0 %copy-start.25 = (bf16[256,256]{1,0:T(8,128)(2,1)S(1)}, bf16[256,256]{1,0:T(8,128)(2,1)}, u32[]{:S(2)}) copy-start(bf16[256,256]{1,0:T(8,128)(2,1)} %get-tuple-element.31) | copy-start | bytes 393220
  126.0 3.6 %copy-start.3 = (f32[256,1280]{0,1:T(8,128)S(1)}, f32[256,1280]{0,1:T(8,128)}, u32[]{:S(2)}) copy-start(f32[256,1280]{0,1:T(8,128)} %get-tuple-element.53) | copy-start | bytes 3932164
  134.3 2.4 %copy-start.15 = (bf16[16,64,1296]{2,1,0:T(8,128)(2,1)S(1)}, bf16[16,64,1296]{2,1,0:T(8,128)(2,1)}, u32[]{:S(2)}) copy-start(bf16[16,64,1296]{2,1,0:T(8,128)(2,1)} %get-tuple-element.21) | copy-start | bytes 7962628
  134.4 2.6 %copy-start.20 = (f32[256,1024]{1,0:T(8,128)S(1)}, f32[256,1024]{1,0:T(8,128)}, u32[]{:S(2)}) copy-start(f32[256,1024]{1,0:T(8,128)} %fusion.81) | copy-start | bytes 3145732
  135.0 3.0 %copy-start.16 = (bf16[256,1280]{0,1:T(8,128)(2,1)}, bf16[256,1280]{0,1:T(8,128)(2,1)S(1)}, u32[]{:S(2)}) copy-start(bf16[256,1280]{0,1:T(8,128)(2,1)S(1)} %get-tuple-element.59) | copy-start | bytes 1966084
  138.1 2.4 %copy-start.5 = (bf16[256,1024]{0,1:T(8,128)(2,1)S(1)}, bf16[256,1024]{0,1:T(8,128)(2,1)}, u32[]{:S(2)}) copy-start(bf16[256,1024]{0,1:T(8,128)(2,1)} %copy.44) | copy-start | bytes 1572868
  138.1 2.4 %copy-start.13 = (f32[256,1024]{0,1:T(8,128)S(1)}, f32[256,1024]{0,1:T(8,128)}, u32[]{:S(2)}) copy-start(f32[256,1024]{0,1:T(8,128)} %copy-done.11) | copy-start | bytes 3145732
  147.2 3.3 %copy-start.8 = (bf16[2,128,2048]{2,1,0:T(8,128)(2,1)S(1)}, bf16[2,128,2048]{2,1,0:T(8,128)(2,1)}, u32[]{:S(2)}) copy-start(bf16[2,128,2048]{2,1,0:T(8,128)(2,1)} %get-tuple-element.20) | copy-start | bytes 3145732
  147.2 3.3 %copy-start.10 = (f32[256,1024]{1,0:T(8,128)S(1)}, f32[256,1024]{1,0:T(8,128)}, u32[]{:S(2)}) copy-start(f32[256,1024]{1,0:T(8,128)} %copy.43) | copy-start | bytes 3145732
  147.2 3.3 %copy-start.24 = (bf16[256,1024]{1,0:T(8,128)(2,1)S(1)}, bf16[256,1024]{1,0:T(8,128)(2,1)}, u32[]{:S(2)}) copy-start(bf16[256,1024]{1,0:T(8,128)(2,1)} %copy-done.23) | copy-start | bytes 1572868
  227.6 4.3 %copy-start.27 = (bf16[2,64,1024]{2,1,0:T(8,128)(2,1)S(1)}, bf16[2,64,1024]{2,1,0:T(8,128)(2,1)}, u32[]{:S(2)}) copy-start(bf16[2,64,1024]{2,1,0:T(8,128)(2,1)} %get-tuple-element.28) | copy-start | bytes 786436
  (23 other events, 30.8 us)

commit v3 on v2

--- a/solution.py
+++ b/solution.py
@@ -37,18 +37,17 @@
     length, channels = conv_in.shape
     heads = step_raw.shape[1]
     width = heads * HEAD_DIM
+    spots = jnp.arange(length)
+    same = segment[:, None] == segment[None, :]
+    gap = spots[:, None] - spots[None, :]
+    moves = jnp.concatenate(
+        [((gap == offset) & same).astype(bf16) for offset in range(1, CONV)], axis=0
+    )
+    moved = jnp.dot(moves, conv_in.astype(bf16), preferred_element_type=bf16)
     summed = tap_bias + conv_in * taps[CONV - 1]
     for offset in range(1, CONV):
-        shifted = jnp.concatenate(
-            [jnp.zeros((offset, channels), f32), conv_in[: length - offset]], axis=0
-        )
-        matched = jnp.concatenate(
-            [
-                jnp.zeros((offset,), f32),
-                (segment[offset:] == segment[: length - offset]).astype(f32),
-            ]
-        )
-        summed = summed + taps[CONV - 1 - offset] * shifted * matched[:, None]
+        shifted = moved[(offset - 1) * length : offset * length].astype(f32)
+        summed = summed + taps[CONV - 1 - offset] * shifted
     active = jax.nn.silu(summed)
     values = active[:, :width].reshape(length, heads, HEAD_DIM).transpose(1, 0, 2)
     input_matrix = active[:, width : width + STATE]

time: 234 us -> 270 us (1.15)
  local copies, waits for them, and re-layouts: 34.4 us -> 56.2 us
  other arithmetic: 31.2 us -> 40.6 us
  matrix products: 35.8 us -> 39.4 us
    reshape x8, local copies, waits for them, and re-layouts: 1.53 us -> 9.29 us  [pick(): array.reshape(lead + (parts, groups, size // (parts * groups)) + tail)]
    another operation x6, other arithmetic: 7.91 us -> 12.9 us
    dynamic_slice x6, local copies, waits for them, and re-layouts: 3.81 us -> 7.28 us  [pick(): chosen = lax.dynamic_index_in_dim(split, group, axis + 1, keepdims=False)]
    another operation x8, local copies, waits for them, and re-layouts: 0.11 us -> 2.91 us
    unnamed x99 -> x137, local copies, waits for them, and re-layouts: 4.98 us -> 5.51 us
where the time goes in v3:
time: 270 us; the launch traced here: 268 us
  Pallas kernels  125 us (46%)
  local copies, waits for them, and re-layouts  56.2 us (21%)
  other arithmetic  40.6 us (15%)
  matrix products  39.4 us (15%)
  blocking collectives  5.66 us (2%)
    pallas_call x1, Pallas kernels, scatter_all(): pl.pallas_call(functools.partial(scatter_kernel, groups, top, mid, count)...  67.3 us
    pallas_call x1, Pallas kernels, gather_all(): pl.pallas_call(functools.partial(gather_kernel, groups, top, mid, count),...  57.4 us
    dot_general x9, matrix products, dot(): return lax.dot_general(left, right, dims, preferred_element_type=f32)  25.1 us
    another operation x6, other arithmetic  12.9 us
    dot_general x6, matrix products, product(): jnp.einsum(spec, left.astype(bf16), right.astype(bf16), preferred_element...  12.7 us
    reshape x8, local copies, waits for them, and re-layouts, pick(): array.reshape(lead + (parts, groups, size // (parts * groups)) + tail)  9.29 us
    dynamic_slice x6, local copies, waits for them, and re-layouts, pick(): chosen = lax.dynamic_index_in_dim(split, group, axis + 1, keepdims=False)  7.28 us
    psum x1, blocking collectives, local(): lax.psum(jnp.stack([jnp.sum(gated * gated, axis=1), jnp.sum(gated * back_...  5.66 us

profile of v3, /device:TPU:0, one launch (start us, length us, event | category | flops | bytes accessed | tf_op | source)
XLA Modules:
  0.0 268.2 jit_solution(12051808819112481746)
XLA Ops:
  4.0 1.8 pad_maximum_fusion.3.refs_0_
  7.9 3.3 %dynamic-slice_reduce_fusion = (bf16[64,16,64]{2,1,0:T(8,128)(2,1)S(1)}, bf16[64,16,64]{2,1,0:T(8,128)(2,1)S(1)}) fusion(bf16[64,16,2,64]{3,2,1,0:T(2,128)(2,1)S(1)} %reshape.404, s32[]{:T(128)S(6)} %select_n.50, bf16[64,16,2,64]{3,2,1,0:T(2,128)(2,1)S(1)} %reshape.400), kind=kLoop, calls=%fused_computation.105 | loop fusion | bytes 524292 | tf_op jit(solution)/shard_map/jit(dynamic_index_in_dim)/dynamic_slice | solution.py:428
  13.6 57.4 %shard_map.203 = (bf16[2,128,2048]{2,1,0:T(8,128)(2,1)}, bf16[16,64,1296]{2,1,0:T(8,128)(2,1)}, bf16[16,64,1024]{2,1,0:T(8,128)(2,1)}, bf16[16,64,1024]{2,1,0:T(8,128)(2,1)}) custom-call(bf16[128,2048]{1,0:T(8,128)(2,1)} %pad_maximum_fusion.3.refs_0_, bf16[64,1296]{1,0:T(8,128)(2,1)} %pad_maximum_fusion.6.refs_1_, bf16[64,1024]{1,0:T(8,128)(2,1)} %reshape.405.refs_2_, ...), custom_call_target="tpu_custom_call" | custom-call | tf_op jit(solution)/shard_map/pallas_call | solution.py:195
  71.0 3.2 %fusion.9 = f32[256,1296]{0,1:T(8,128)S(1)} fusion(bf16[1024,1296]{1,0:T(8,128)(2,1)} %bitcast.155, bf16[256,2048]{1,0:T(8,128)(2,1)} %bitcast.141), kind=kOutput, calls=%fused_computation.16 | convolution fusion | flops 680140800 | bytes 4734976 | tf_op jit(solution)/shard_map/dot_general | solution.py:24
  77.7 1.5 reshape.415
  79.1 1.6 dynamic-slice_reduce_fusion.2
  80.7 1.4 reshape.416
  82.1 1.5 fusion.77
  92.4 3.9 %fusion.93 = (bf16[256,1280]{0,1:T(8,128)(2,1)S(1)}, f32[256,1280]{0,1:T(8,128)}, f32[256,1280]{0,1:T(8,128)}) fusion(bf16[768,1280]{0,1:T(8,128)(2,1)S(1)} %fusion.41, f32[1280]{0:T(1024)} %get-tuple-element.44, f32[1280]{0:T(1024)} %get-tuple-element.45, f32[1280]{0:T(1024)} %get-tuple-element.43, f32[1280]{0:T(1024)} %get-tuple-element.42, ...), kind=kLoop, calls=%fused_computation.201 | loop fusion | flops 5242880 | bytes 6579200 | tf_op jit(solution)/shard_map/convert.15
  106.4 1.9 reduce-window.14
  108.3 1.4 slice_reduce_fusion.2
  113.9 1.6 fusion.28
  116.6 2.5 copy.50
  119.1 3.5 %fusion.49 = f32[256,1024]{1,0:T(8,128)} fusion(bf16[1024,1024]{1,0:T(8,128)(2,1)} %bitcast.160, bf16[256,2048]{1,0:T(8,128)(2,1)} %bitcast.142), kind=kOutput, calls=%fused_computation.112 | convolution fusion | flops 536870912 | bytes 3670016 | tf_op jit(solution)/shard_map/dot_general | solution.py:24
  124.0 4.0 %multiply_reduce_fusion.4 = (f32[256]{0:T(256)S(1)}, f32[256]{0:T(256)S(1)}, bf16[256,1024]{1,0:T(8,128)(2,1)}) fusion(f32[256,1024]{1,0:T(8,128)} %copy.50, f32[256,1024]{1,0:T(8,128)} %fusion.49, f32[1024]{0:T(1024)} %mul.344, bf16[1024,1024]{1,0:T(8,128)(2,1)} %bitcast.158, bf16[256,2048]{1,0:T(8,128)(2,1)} %bitcast.143), kind=kOutput, calls=%fused_computation.85 | convolution fusion | flops 540016128 | bytes 5249024 | tf_op jit(solution)/shard_map/dot_general | solution.py:24
  128.6 5.7 %psum.7 = f32[2,256]{1,0:T(2,128)} all-reduce(f32[2,256]{1,0:T(2,128)} %pad_maximum_fusion.10), channel_id=1, replica_groups=mesh['seq'=2,'fsdp'=16] {'seq'}, use_global_device_ids=true, to_apply=%region_5.6 | all-reduce | flops 512 | bytes 4096 | tf_op jit(solution)/shard_map/psum | solution.py:497
  135.0 3.9 %convolution_convert_fusion.6 = bf16[256,1024]{1,0:T(8,128)(2,1)} fusion(bf16[1024,1024]{1,0:T(8,128)(2,1)} %bitcast.161, f32[256]{0:T(256)S(1)} %bitcast.173, f32[1024]{0:T(1024)} %mul.344, f32[256,1024]{1,0:T(8,128)} %copy.50, bf16[256,1024]{1,0:T(8,128)(2,1)} %get-tuple-element.76), kind=kOutput, calls=%fused_computation.60 | convolution fusion | flops 539492352 | bytes 4199424 | tf_op jit(solution)/shard_map/dot_general | solution.py:24
  139.0 2.2 multiply_convert_fusion.15
  142.0 1.7 fusion.99
  143.8 2.1 copy.51
  145.9 4.4 %fusion.34 = (f32[16,256]{1,0:T(8,128)}, bf16[16,256,64]{1,2,0:T(8,128)(2,1)}) fusion(f32[256,1280]{0,1:T(8,128)} %get-tuple-element.52, bf16[16,256,64]{1,2,0:T(8,128)(2,1)} %bitcast.138, f32[256,256]{1,0:T(8,128)} %fusion.60, f32[16,256]{1,0:T(8,128)} %copy-done.55, pred[256,256]{1,0:T(8,128)(4,1)} %get-tuple-element.72), kind=kOutput, calls=%fused_computation.71 | convolution fusion | flops 140505088 | bytes 2473984 | tf_op jit(solution)/shard_map/transpose(jvp(hij,hjp->hip))/dot_general | solution.py:33
  150.2 3.9 %fusion.6 = (f32[16,256]{1,0:T(8,128)S(1)}, f32[16,256]{1,0:T(8,128)S(1)}, bf16[256,256]{1,0:T(8,128)(2,1)}) fusion(f32[256,256]{1,0:T(8,128)S(1)} %copy-done.30, f32[16,256]{1,0:T(8,128)S(1)} %copy-done.56, pred[256,256]{1,0:T(8,128)(4,1)S(1)} %copy-done.45, bf16[16,256,64]{1,2,0:T(8,128)(2,1)S(1)} %bitcast.139, f32[16,256,64]{1,2,0:T(8,128)S(1)} %bitcast.151, ...), kind=kOutput, calls=%fused_computation.11 | convolution fusion | flops 148299776 | bytes 2097152 | tf_op jit(solution)/shard_map/transpose(jvp(hij,hjp->hip))/dot_general | solution.py:33
  154.7 3.8 %reduce-window.16 = f32[16,2,128]{2,0,1:T(8,128)} reduce-window(f32[16,2,128]{2,0,1:T(8,128)} %copy_bitcast_fusion.1, f32[]{:T(128)} %constant.73.clone.1), window={size=1x1x128 pad=0_0x0_0x0_127}, to_apply=%region_10.11 | reduce-window | flops 520192 | bytes 32772 | tf_op jit(solution)/shard_map/reduce-window.2
  161.9 1.6 fusion.90
  163.5 1.5 fusion.30
  167.1 1.8 fusion.89
  177.4 2.1 convolution_convert_fusion
  179.5 3.1 %copy.59 = bf16[1024,1296]{1,0:T(8,128)(2,1)} copy(bf16[1024,1296]{0,1:T(8,128)(2,1)S(1)} %convolution_convert_fusion) | data formatting | bytes 5308416 | tf_op jit(solution)/shard_map/convert_element_type | solution.py:519
  182.7 3.3 %convolution_convert_fusion.4 = bf16[1024,1024]{1,0:T(8,128)(2,1)} fusion(bf16[256,1024]{1,0:T(8,128)(2,1)S(1)} %copy-done.3, bf16[256,2048]{1,0:T(8,128)(2,1)} %bitcast.145), kind=kOutput, calls=%fused_computation.27 | convolution fusion | flops 537919488 | bytes 3145728 | tf_op jit(solution)/shard_map/dot_general | solution.py:24
  186.0 2.4 convolution_convert_fusion.3
  188.4 67.3 %shard_map.204 = (bf16[2,256,1024]{2,1,0:T(8,128)(2,1)}, f32[120,128]{1,0:T(8,128)}, bf16[2,64,1296]{2,1,0:T(8,128)(2,1)}, bf16[2,64,1024]{2,1,0:T(8,128)(2,1)}, bf16[2,64,1024]{2,1,0:T(8,128)(2,1)}) custom-call(bf16[2,256,1024]{2,1,0:T(8,128)(2,1)} %pad_maximum_fusion.1.refs_0_, f32[120,128]{1,0:T(8,128)} %pad_bitcast_fusion.refs_1_, ...), custom_call_target="tpu_custom_call" | custom-call | tf_op jit(solution)/shard_map/pallas_call | solution.py:377
  255.7 1.6 convert_reduce_fusion
  (255 shorter events, 63.8 us)
Async XLA Ops:
  0.6 12.3 %copy-start = (bf16[128,1024]{1,0:T(8,128)(2,1)S(1)}, bf16[128,1024]{1,0:T(8,128)(2,1)}, u32[]{:S(2)}) copy-start(bf16[128,1024]{1,0:T(8,128)(2,1)} %param.23) | copy-start | bytes 786436
  0.7 6.1 %copy-start.22 = (bf16[64,4384]{1,0:T(8,128)(2,1)S(1)}, bf16[64,4384]{1,0:T(8,128)(2,1)}, u32[]{:S(2)}) copy-start(bf16[64,4384]{1,0:T(8,128)(2,1)} %param.15) | copy-start | bytes 1683460
  6.8 4.6 %slice-start = ((bf16[64,4384]{1,0:T(8,128)(2,1)}), bf16[64,256]{1,0:T(8,128)(2,1)S(1)}, s32[]{:S(2)}) async-start(bf16[64,4384]{1,0:T(8,128)(2,1)} %param.15), calls=%async_computation | async-start | bytes 65536 | tf_op jit(solution)/shard_map/slice | solution.py:448
  71.0 3.2 %copy-start.60 = (s32[1,256]{1,0:T(1,128)S(1)}, s32[1,256]{1,0:T(1,128)}, u32[]{:S(2)}) copy-start(s32[1,256]{1,0:T(1,128)} %param.14) | copy-start | bytes 3076
  111.0 2.9 %copy-start.44 = (pred[256,256]{1,0:T(8,128)(4,1)S(1)}, pred[256,256]{1,0:T(8,128)(4,1)}, u32[]{:S(2)}) copy-start(pred[256,256]{1,0:T(8,128)(4,1)} %get-tuple-element.72) | copy-start | bytes 196612
  111.0 2.9 %copy-start.64 = (f32[16]{0:T(128)S(1)}, f32[16]{0:T(128)}, u32[]{:S(2)}) copy-start(f32[16]{0:T(128)} %get-tuple-element.84) | copy-start | bytes 196
  112.5 2.9 %copy-start.55 = (f32[16,256]{1,0:T(8,128)}, f32[16,256]{1,0:T(8,128)S(1)}, u32[]{:S(2)}) copy-start(f32[16,256]{1,0:T(8,128)S(1)} %copy_bitcast_fusion) | copy-start | bytes 49156
  135.0 3.9 %copy-start.57 = (f32[1,256]{1,0:T(1,128)}, f32[1,256]{1,0:T(1,128)S(1)}, u32[]{:S(2)}) copy-start(f32[1,256]{1,0:T(1,128)S(1)} %get-tuple-element.71) | copy-start | bytes 3076
  135.0 3.9 %copy-start.6 = (f32[256,1024]{1,0:T(8,128)S(1)}, f32[256,1024]{1,0:T(8,128)}, u32[]{:S(2)}) copy-start(f32[256,1024]{1,0:T(8,128)} %fusion.49) | copy-start | bytes 3145732
  135.0 3.9 %copy-start.9 = (f32[256,1024]{1,0:T(8,128)S(1)}, f32[256,1024]{1,0:T(8,128)}, u32[]{:S(2)}) copy-start(f32[256,1024]{1,0:T(8,128)} %copy.50) | copy-start | bytes 3145732
  135.0 3.9 %copy-start.23 = (bf16[256,1024]{1,0:T(8,128)(2,1)S(1)}, bf16[256,1024]{1,0:T(8,128)(2,1)}, u32[]{:S(2)}) copy-start(bf16[256,1024]{1,0:T(8,128)(2,1)} %get-tuple-element.76) | copy-start | bytes 1572868
  135.0 3.9 %copy-start.52 = (f32[1024]{0:T(1024)S(1)}, f32[1024]{0:T(1024)}, u32[]{:S(2)}) copy-start(f32[1024]{0:T(1024)} %mul.344) | copy-start | bytes 12292
  138.9 3.1 %copy-start.17 = (bf16[16,64,1024]{2,1,0:T(8,128)(2,1)S(1)}, bf16[16,64,1024]{2,1,0:T(8,128)(2,1)}, u32[]{:S(2)}) copy-start(bf16[16,64,1024]{2,1,0:T(8,128)(2,1)} %get-tuple-element.22) | copy-start | bytes 6291460
  145.8 4.4 %copy-start.4 = (bf16[256,1024]{0,1:T(8,128)(2,1)S(1)}, bf16[256,1024]{0,1:T(8,128)(2,1)}, u32[]{:S(2)}) copy-start(bf16[256,1024]{0,1:T(8,128)(2,1)} %copy.51) | copy-start | bytes 1572868
  145.8 4.4 %copy-start.12 = (f32[256,1024]{0,1:T(8,128)S(1)}, f32[256,1024]{0,1:T(8,128)}, u32[]{:S(2)}) copy-start(f32[256,1024]{0,1:T(8,128)} %copy-done.11) | copy-start | bytes 3145732
  145.8 4.4 %copy-start.30 = (f32[256,256]{1,0:T(8,128)S(1)}, f32[256,256]{1,0:T(8,128)}, u32[]{:S(2)}) copy-start(f32[256,256]{1,0:T(8,128)} %fusion.60) | copy-start | bytes 786436
  145.8 4.4 %copy-start.38 = (f32[256,16]{0,1:T(8,128)S(1)}, f32[256,16]{0,1:T(8,128)}, u32[]{:S(2)}) copy-start(f32[256,16]{0,1:T(8,128)} %get-tuple-element.50) | copy-start | bytes 49156
  145.8 4.4 %copy-start.45 = (pred[256,256]{1,0:T(8,128)(4,1)S(1)}, pred[256,256]{1,0:T(8,128)(4,1)}, u32[]{:S(2)}) copy-start(pred[256,256]{1,0:T(8,128)(4,1)} %get-tuple-element.72) | copy-start | bytes 196612
  145.8 4.4 %copy-start.56 = (f32[16,256]{1,0:T(8,128)S(1)}, f32[16,256]{1,0:T(8,128)}, u32[]{:S(2)}) copy-start(f32[16,256]{1,0:T(8,128)} %copy-done.55) | copy-start | bytes 49156
  161.1 3.8 %copy-start.25 = (bf16[256,256]{1,0:T(8,128)(2,1)S(1)}, bf16[256,256]{1,0:T(8,128)(2,1)}, u32[]{:S(2)}) copy-start(bf16[256,256]{1,0:T(8,128)(2,1)} %get-tuple-element.34) | copy-start | bytes 393220
  161.1 5.9 %copy-start.1 = (f32[256,1280]{0,1:T(8,128)S(1)}, f32[256,1280]{0,1:T(8,128)}, u32[]{:S(2)}) copy-start(f32[256,1280]{0,1:T(8,128)} %get-tuple-element.53) | copy-start | bytes 3932164
  163.5 7.2 %copy-start.49 = (bf16[256,16]{0,1:T(8,128)(2,1)}, bf16[256,16]{0,1:T(8,128)(2,1)S(1)}, u32[]{:S(2)}) copy-start(bf16[256,16]{0,1:T(8,128)(2,1)S(1)} %get-tuple-element.47) | copy-start | bytes 24580
  173.5 2.9 %copy-start.43 = (f32[1024]{0:T(1024)S(1)}, f32[1024]{0:T(1024)}, u32[]{:S(2)}) copy-start(f32[1024]{0:T(1024)} %param.21) | copy-start | bytes 12292
  173.5 2.9 %copy-start.54 = (f32[1024]{0:T(1024)S(1)}, f32[1024]{0:T(1024)}, u32[]{:S(2)}) copy-start(f32[1024]{0:T(1024)} %get-tuple-element.56) | copy-start | bytes 12292
  173.5 3.9 %copy-start.50 = (bf16[256,16]{0,1:T(8,128)(2,1)S(1)}, bf16[256,16]{0,1:T(8,128)(2,1)}, u32[]{:S(2)}) copy-start(bf16[256,16]{0,1:T(8,128)(2,1)} %copy-done.49) | copy-start | bytes 24580
  179.5 3.2 %copy-start.3 = (bf16[256,1024]{1,0:T(8,128)(2,1)S(1)}, bf16[256,1024]{1,0:T(8,128)(2,1)}, u32[]{:S(2)}) copy-start(bf16[256,1024]{1,0:T(8,128)(2,1)} %copy-done.2) | copy-start | bytes 1572868
  182.6 3.3 %copy-start.8 = (bf16[2,128,2048]{2,1,0:T(8,128)(2,1)S(1)}, bf16[2,128,2048]{2,1,0:T(8,128)(2,1)}, u32[]{:S(2)}) copy-start(bf16[2,128,2048]{2,1,0:T(8,128)(2,1)} %get-tuple-element.20) | copy-start | bytes 3145732
  182.6 3.3 %copy-start.10 = (f32[256,1024]{1,0:T(8,128)S(1)}, f32[256,1024]{1,0:T(8,128)}, u32[]{:S(2)}) copy-start(f32[256,1024]{1,0:T(8,128)} %copy.50) | copy-start | bytes 3145732
  182.6 3.3 %copy-start.24 = (bf16[256,1024]{1,0:T(8,128)(2,1)S(1)}, bf16[256,1024]{1,0:T(8,128)(2,1)}, u32[]{:S(2)}) copy-start(bf16[256,1024]{1,0:T(8,128)(2,1)} %get-tuple-element.76) | copy-start | bytes 1572868
  182.6 3.3 %copy-start.53 = (f32[1024]{0:T(1024)S(1)}, f32[1024]{0:T(1024)}, u32[]{:S(2)}) copy-start(f32[1024]{0:T(1024)} %mul.344) | copy-start | bytes 12292
  182.7 3.3 %copy-start.58 = (f32[1,256]{1,0:T(1,128)S(1)}, f32[1,256]{1,0:T(1,128)}, u32[]{:S(2)}) copy-start(f32[1,256]{1,0:T(1,128)} %copy-done.57) | copy-start | bytes 3076
  262.1 5.2 %copy-start.27 = (bf16[2,64,1024]{2,1,0:T(8,128)(2,1)S(1)}, bf16[2,64,1024]{2,1,0:T(8,128)(2,1)}, u32[]{:S(2)}) copy-start(bf16[2,64,1024]{2,1,0:T(8,128)(2,1)} %get-tuple-element.28) | copy-start | bytes 786436
  (37 other events, 61.6 us)
